TPU v7x, 256 devices: a whole 4x4x8 slice. The times are simulated.
256 devices in a mesh: prow: 8 (over z_hi, y), pcol: 32 (over x, z_lo, core).
Axes of the slice: x: 4, y: 4, z: 8 (z_hi: 2, z_lo: 4; z = z_hi * 4 + z_lo), core: 2. Of those that a mesh axis runs over, the one named last changes fastest.
Arguments:
- inverse_blocks: float32 [12288, 12288], P('pcol', 'prow')
- panel_first: float32 [12288, 384], P('prow'), may hold values from -0.0546875 to 0.0546875
- panel_second: float32 [12288, 384], P('pcol'), may hold values from -0.0546875 to 0.0546875
- panel_link: float32 [384, 384], replicated, may hold values from -0.3125 to 0.3125
- diag_inverse: float32 [384, 384], replicated
- ancestors: int32 [2, 32], replicated, may hold values from 0 to 1, as said below
Outputs:
- column_first: float32 [12288, 384], P('pcol')
- diag_first: float32 [384, 384], replicated
- column_second: float32 [12288, 384], P(('prow', 'pcol'))
- corner: float32 [384, 384], replicated
Inputs may be any that keep to these rules, and one draw needn't show every extreme that they name: `ancestors`: every block marked in row 1 is also marked in row 0; `inverse_blocks` is symmetric (equal to its transpose).
All inputs are finite; a program needn't handle non-finite values.
Results may differ from a plain program's by a relative error of at most 0.0001.
Values sent between devices are 32-bit elements; how exact they have to be, the bound alone decides.
A program may use at most 64 MiB of HBM per device.

v0:
```python
import jax
import jax.numpy as jnp
from jax import lax
from jax.sharding import PartitionSpec as P


def product(left, right):
    return jnp.dot(left, right, precision=lax.Precision.HIGHEST, preferred_element_type=jnp.float32)


def inner_rows(left, right):
    return lax.dot_general(
        left,
        right,
        (((0,), (0,)), ((), ())),
        precision=lax.Precision.HIGHEST,
        preferred_element_type=jnp.float32,
    )


def body(inverse_blocks, panel_first, panel_second, panel_link, diag_inverse, ancestors):
    order = panel_link.shape[0]
    columns = lax.axis_size("pcol")
    blocks_here = inverse_blocks.shape[1] // order
    col = lax.axis_index("pcol")
    row = lax.axis_index("prow")
    marks = ancestors.astype(jnp.float32)
    pick = (jnp.arange(columns) == col).astype(jnp.float32)
    mark_first = jnp.sum(marks[0] * pick)
    mark_second = jnp.sum(marks[1] * pick)
    first_rows = jnp.repeat(
        lax.dynamic_slice_in_dim(marks[0], row * blocks_here, blocks_here), order
    )[:, None]
    partial_value = product(inverse_blocks, first_rows * panel_first)
    owner = (col // blocks_here == row).astype(jnp.float32)
    local = jnp.clip(col - row * blocks_here, 0, blocks_here - 1)
    panel_own = owner * lax.dynamic_slice_in_dim(panel_first, local * order, order, 0)
    summed, panel_block = lax.psum((partial_value, panel_own), "prow")
    column_first = -mark_first * summed
    diag_term = owner * product(column_first, panel_link)
    placed = lax.dynamic_update_slice_in_dim(
        jnp.zeros((blocks_here * order, order), jnp.float32), diag_term, local * order, 0
    )
    scaled_panel = mark_second * panel_second
    piece = blocks_here * order // columns
    reduced = lax.psum_scatter(
        inner_rows(inverse_blocks, scaled_panel) + placed, "pcol", scatter_dimension=0, tiled=True
    )
    row_start = row * blocks_here * order + col * piece
    row_block = (row_start + jnp.arange(piece)) // order
    onehot = (row_block[:, None] == jnp.arange(columns)[None, :]).astype(jnp.float32)
    second_rows = jnp.sum(onehot * marks[1][None, :], axis=1)
    column_second = -second_rows[:, None] * reduced
    block_coupling = inner_rows(panel_block, column_first)
    diag_first = diag_inverse - lax.psum(block_coupling, "pcol")
    cross = lax.psum(mark_second * inner_rows(column_first, panel_second), "pcol")
    corner = -(cross + product(diag_first, panel_link))
    return (column_first, diag_first, column_second, corner)


def solution(mesh):
    placed = (P("pcol", "prow"), P("prow", None), P("pcol", None), P(), P(), P())
    return jax.shard_map(
        body,
        mesh=mesh,
        in_specs=placed,
        out_specs=(P("pcol", None), P(), P(("prow", "pcol"), None), P()),
        check_vma=False,
    )
```

profile of v0, /device:TPU:1, one launch (start us, length us, event | category | flops | bytes accessed | tf_op | source)
XLA Modules:
  0.0 575.7 jit_solution(8268338701713306882)
XLA Ops:
  7.2 0.0 copy-start
  7.2 0.0 copy-start.4
  7.2 0.0 all-reduce.7.cloned.1.call-start
  7.3 1.3 constant_dynamic-slice_fusion
  8.5 0.2 copy.25
  8.8 0.0 copy-done.4
  8.8 0.1 fusion.12
  8.9 0.1 broadcast_in_dim.2
  8.9 0.9 broadcast_multiply_fusion
  9.8 0.0 copy-done
  9.8 10.2 %fusion.5 = f32[384,384]{0,1:T(8,128)} fusion(f32[384,1536]{1,0:T(8,128)S(1)} %copy-done, f32[1536,384]{1,0:T(8,128)} %param.7, f32[1536]{0:T(1024)S(1)} %mul.78), kind=kOutput, calls=%fused_computation.8 | convolution fusion | flops 2718498816 | bytes 5314560 | tf_op jit(solution)/shard_map/dot_general | solution.py:8
  20.0 0.0 copy-start.2
  20.0 0.0 all-reduce.7.cloned.1.call-update
  20.1 0.0 all-reduce.5.cloned.1.call-start
  20.1 0.6 fusion.14
  21.4 112.7 %all-reduce.7.cloned.1.call-done = (f32[384,384]{0,1:T(8,128)}, f32[384,384]{0,1:T(8,128)}) async-done(((f32[384,384]{0,1:T(8,128)}, f32[384,384]{0,1:T(8,128)}), (f32[384,384]{0,1:T(8,128)}, f32[384,384]{0,1:T(8,128)})) %all-reduce.7.cloned.1.call-update) | async-done | bytes 1179664 | tf_op jit(solution)/shard_map/psum | solution.py:38
  134.1 1.1 broadcast_multiply_fusion.1
  135.2 3.1 fusion.15
  138.3 0.0 copy-done.2
  138.3 2.7 convolution_multiply_fusion
  141.0 0.0 all-reduce.5.cloned.1.call-update
  141.1 0.2 reduce-scatter.4.cloned.1.call-start
  141.3 4.6 fusion.9
  145.9 0.0 copy-start.3
  145.9 1.4 copy.30
  147.3 0.0 copy-done.3
  147.4 2.2 fusion.3
  149.6 3.1 copy.23
  152.6 0.0 reduce-scatter.4.cloned.1.call-update
  152.7 0.1 select_reduce_fusion
  152.8 1.0 copy.20
  153.8 265.1 %all-reduce.5.cloned.1.call-done = (f32[384,384]{1,0:T(8,128)}, f32[384,384]{1,0:T(8,128)}) async-done(((f32[384,384]{1,0:T(8,128)}, f32[384,384]{1,0:T(8,128)}), (f32[384,384]{1,0:T(8,128)}, f32[384,384]{1,0:T(8,128)})) %all-reduce.5.cloned.1.call-update) | async-done | bytes 1179664 | tf_op jit(solution)/shard_map/psum | solution.py:55
  418.9 1.3 sub.18
  420.2 0.0 copy-start.1
  420.3 3.4 fusion.4
  423.6 143.8 %reduce-scatter.4.cloned.1.call-done = f32[48,384]{1,0:T(8,128)} async-done(((f32[1536,384]{1,0:T(8,128)}), f32[48,384]{1,0:T(8,128)}) %reduce-scatter.4.cloned.1.call-update) | async-done | bytes 73744
  567.4 1.0 copy.24
  568.5 0.7 copy.21
  569.2 0.0 copy-done.1
  (6 shorter events, 0.1 us)
Async XLA Ops:
  7.2 2.6 copy-start
  7.2 1.6 copy-start.4
  7.2 126.9 %all-reduce.7.cloned.1.call-start = ((), (), s32[]{:S(2)}) async-start(), calls=%async_computation.3 | async-start | bytes 2359296 | tf_op jit(solution)/shard_map/psum | solution.py:38
  20.0 118.3 %copy-start.2 = (f32[384,384]{1,0:T(8,128)S(1)}, f32[384,384]{1,0:T(8,128)}, u32[]{:S(2)}) copy-start(f32[384,384]{1,0:T(8,128)} %param.8) | copy-start | bytes 1769476
  20.1 398.9 %all-reduce.5.cloned.1.call-start = ((), (), s32[]{:S(2)}) async-start(), calls=%async_computation.2 | async-start | bytes 2359296 | tf_op jit(solution)/shard_map/psum | solution.py:55
  141.1 426.4 %reduce-scatter.4.cloned.1.call-start = ((), (), s32[]{:S(2)}) async-start(), calls=%async_computation.1 | async-start | bytes 2433024
  145.9 1.4 copy-start.3
  420.2 149.0 %copy-start.1 = (f32[384,384]{1,0:T(8,128)}, f32[384,384]{1,0:T(8,128)S(1)}, u32[]{:S(2)}) copy-start(f32[384,384]{1,0:T(8,128)S(1)} %sub.18) | copy-start | bytes 1769476
Sparse Core Ops, SparseCore 0:
  20.2 113.8 all-reduce.6
  141.2 277.7 all-reduce.4
  421.5 145.9 reduce-scatter.3
where the time goes:
time: 580 us; the launch traced here: 576 us
  waiting for transfers between devices  522 us (90%)
  matrix products  26.3 us (5%)
  between operations  14.5 us (2%)
  local copies, waits for them, and re-layouts  9 us (2%)
    psum x1, waiting for transfers between devices, body(): diag_first = diag_inverse - lax.psum(block_coupling, 'pcol')  265 us
    unnamed x4, waiting for transfers between devices  144 us
    psum x1, waiting for transfers between devices, body(): summed, panel_block = lax.psum((partial_value, panel_own), 'prow')  113 us
    dot_general x3, matrix products, product(): jnp.dot(left, right, precision=lax.Precision.HIGHEST, preferred_element_t...  15.8 us
  transfers between devices with their start and end apart: 3, of which 3 were waited for; matrix products, arithmetic and copies ran while one was open for 3% of the time, Pallas kernels for 0%

commit v1 on v0

v1 whole, which is shorter than its diff:
```python
import functools

import jax
import jax.numpy as jnp
from jax import lax
from jax.experimental import pallas as pl
from jax.experimental.pallas import tpu as pltpu
from jax.sharding import PartitionSpec as P

MESH = pl.DeviceIdType.MESH
F32 = jnp.float32
BF16 = jnp.bfloat16
B = 384
CH = 3
W = 128
H = 48
S = 16
ROWS = (((0,), (0,)), ((), ()))
PLAIN = (((1,), (0,)), ((), ()))


def split(value):
    high = value.astype(BF16)
    low = (value - high.astype(F32)).astype(BF16)
    return high, low


def mul(left, right, dims=PLAIN):
    return lax.dot_general(left, right, dims, preferred_element_type=F32)


def product(left, right, dims=PLAIN):
    left_high, left_low = left
    right_high, right_low = right
    return mul(left_high, right_high, dims) + (mul(left_high, right_low, dims) + mul(left_low, right_high, dims))


class Copies:
    def __init__(self, send_sems, recv_sems):
        self.send_sems, self.recv_sems = send_sems, recv_sems
        self.sends, self.recvs, self.sent = {}, {}, []

    def slot(self, table, key):
        if key not in table:
            table[key] = len(table)
        return table[key]

    def make(self, key, src, dst, device, send_key=None):
        send = self.slot(self.sends, key if send_key is None else send_key)
        recv = self.slot(self.recvs, key)
        return pltpu.make_async_remote_copy(
            src_ref=src,
            dst_ref=dst,
            send_sem=self.send_sems.at[send],
            recv_sem=self.recv_sems.at[recv],
            device_id=device,
            device_id_type=MESH,
        )

    def send(self, key, src, dst, device):
        copy = self.make(key, src, dst, device)
        copy.start()
        self.sent.append(copy)

    def wait(self, key, dst, device):
        self.make(key, dst, dst, device).wait_recv()

    def finish(self):
        for copy in self.sent:
            copy.wait_send()


class Ring:
    def __init__(self, copies, name, pos, plus, minus, get):
        self.copies, self.name, self.pos, self.plus, self.minus, self.get = copies, name, pos, plus, minus, get

    def at(self, offset, half):
        return self.get(lax.rem(self.pos + offset, 4), half)


class Scatter(Ring):
    def __init__(self, copies, name, pos, plus, minus, get, relay, direct, final):
        super().__init__(copies, name, pos, plus, minus, get)
        self.relayed, self.direct, self.final = relay, direct, final

    def start_far(self):
        self.copies.send((self.name, 0), self.at(2, 0), self.relayed(0), self.plus)
        self.copies.send((self.name, 1), self.at(2, 1), self.relayed(1), self.minus)

    def start_plus(self):
        self.copies.send((self.name, 2), self.at(1, 1), self.direct(0), self.plus)

    def start_minus(self):
        self.copies.send((self.name, 3), self.at(3, 0), self.direct(1), self.minus)

    def relay(self):
        self.copies.wait((self.name, 0), self.relayed(0), self.minus)
        mine = self.at(1, 0)
        mine[...] = mine[...] + self.relayed(0)[...]
        self.copies.send((self.name, 4), mine, self.final(0), self.plus)
        self.copies.wait((self.name, 1), self.relayed(1), self.plus)
        mine = self.at(3, 1)
        mine[...] = mine[...] + self.relayed(1)[...]
        self.copies.send((self.name, 5), mine, self.final(1), self.minus)

    def finish(self):
        self.copies.wait((self.name, 2), self.direct(0), self.minus)
        self.copies.wait((self.name, 3), self.direct(1), self.plus)
        self.copies.wait((self.name, 4), self.final(0), self.minus)
        self.copies.wait((self.name, 5), self.final(1), self.plus)
        first = self.at(0, 0)[...] + (self.direct(1)[...] + self.final(0)[...])
        second = self.at(0, 1)[...] + (self.direct(0)[...] + self.final(1)[...])
        return first, second


class Gather(Ring):
    def start(self):
        for number, half, device in ((0, 0, self.plus), (1, 1, self.minus), (2, 1, self.plus), (3, 0, self.minus)):
            self.copies.send((self.name, number), self.at(0, half), self.at(0, half), device)

    def relay(self):
        self.copies.wait((self.name, 0), self.at(3, 0), self.minus)
        self.copies.send((self.name, 4), self.at(3, 0), self.at(3, 0), self.plus)
        self.copies.wait((self.name, 1), self.at(1, 1), self.plus)
        self.copies.send((self.name, 5), self.at(1, 1), self.at(1, 1), self.minus)

    def near(self):
        self.copies.wait((self.name, 2), self.at(3, 1), self.minus)
        self.copies.wait((self.name, 3), self.at(1, 0), self.plus)

    def far(self):
        self.copies.wait((self.name, 4), self.at(2, 0), self.minus)
        self.copies.wait((self.name, 5), self.at(2, 1), self.plus)


def kernel(
    marks, inv, pan1, pan2, link, diag, column_first, diag_first, column_second, corner,
    inv_high, inv_low, pan1_cat, pan2_cat, link_high, link_low, base,
    part, part_relay, part_direct, part_final, quarter, quarter_in, column,
    wide, wide_in, wide_relay, wide_direct, wide_final, mine, mine_in, link_rows,
    turned, turned_in, cross, pair, pair_in, slices, slices_in, depth, grid,
    send_sems, recv_sems,
):
    row, col = lax.axis_index("prow"), lax.axis_index("pcol")
    y, zh = lax.rem(row, 4), lax.div(row, 4)
    x, zl, core = lax.div(col, 8), lax.rem(lax.div(col, 2), 4), lax.rem(col, 2)
    z = zh * 4 + zl

    def device(y=y, zh=zh, x=x, zl=zl, core=core):
        return (zh * 4 + y, (x * 4 + zl) * 2 + core)

    def turn(value, step, size=4):
        return lax.rem(value + step, size)

    def along_z(step):
        there = turn(z, step, 8)
        return device(zh=lax.div(there, 4), zl=lax.rem(there, 4))

    y_plus, y_minus = device(y=turn(y, 1)), device(y=turn(y, 3))
    x_plus, x_minus, x_far = device(x=turn(x, 1)), device(x=turn(x, 3)), device(x=turn(x, 2))
    partner = device(core=1 - core)
    owner_row = lax.div(col, 4)
    is_owner = row == owner_row

    gives = zh == lax.div(col, 16)

    def taker(half):
        return (owner_row, lax.rem(col, 4) * 8 + y * 2 + half)

    def is_self(half):
        there = taker(half)
        return jnp.logical_and(there[0] == row, there[1] == col)

    giver = (zh * 4 + lax.div(lax.rem(col, 8), 2), row * 4 + lax.div(col, 8))
    from_self = jnp.logical_and(giver[0] == row, giver[1] == col)

    barrier = pltpu.get_barrier_semaphore()

    def greet(there):
        pl.semaphore_signal(barrier, inc=1, device_id=there, device_id_type=MESH)

    for there in (y_plus, y_minus, x_plus, x_minus, x_far, partner):
        greet(there)
    for step in range(1, 8):
        greet(along_z(step))

    @pl.when(jnp.logical_not(from_self))
    def _():
        greet(giver)

    @pl.when(jnp.logical_not(is_owner))
    def _():
        greet((owner_row, col))

    copies = Copies(send_sems, recv_sems)

    first_own = marks[0, col].astype(F32)
    second_own = marks[1, col].astype(F32)
    for block in range(4):
        at = pl.ds(block * B, B)
        scaled = pan1[at, :] * marks[0, row * 4 + block].astype(F32)
        high, low = split(scaled)
        for chunk in range(CH):
            lanes = slice(chunk * W, (chunk + 1) * W)
            pan1_cat[chunk, at, 0:W] = high[:, lanes]
            pan1_cat[chunk, at, W : 2 * W] = low[:, lanes]
        inv_high[:, at], inv_low[:, at] = split(inv[:, at])

    ring = []
    for chunk in range(CH):
        ring.append(
            Scatter(
                copies, ("part", chunk), y, y_plus, y_minus,
                lambda q, h, chunk=chunk: part.at[chunk, q, h],
                lambda h, chunk=chunk: part_relay.at[chunk, h],
                lambda h, chunk=chunk: part_direct.at[chunk, h],
                lambda h, chunk=chunk: part_final.at[chunk, h],
            )
        )

    def partial_product(chunk):
        both = mul(inv_high[...], pan1_cat[chunk])
        rest = mul(inv_low[...], pan1_cat[chunk, :, 0:W])
        total = (both[:, 0:W] + (both[:, W : 2 * W] + rest)) * (-first_own)
        part[chunk] = total.reshape(4, 2, H, W)

    def start_ring(chunk):
        ring[chunk].start_far()
        ring[chunk].start_plus()
        ring[chunk].start_minus()

    partial_product(0)
    waits = 13 + jnp.where(is_owner, 7, 0)
    for half in range(2):
        waits = waits + jnp.where(jnp.logical_and(gives, jnp.logical_not(is_self(half))), 1, 0)
    pl.semaphore_wait(barrier, waits)
    start_ring(0)
    partial_product(1)
    start_ring(1)
    partial_product(2)
    start_ring(2)

    high, low = split(pan2[...] * second_own)
    pan2_cat[:, 0:B] = high
    pan2_cat[:, B : 2 * B] = low

    def wide_product(there):
        at = pl.ds(pl.multiple_of(there * B, B), B)
        both = mul(inv_high[:, at], pan2_cat[...], ROWS)
        rest = mul(inv_low[:, at], pan2_cat[:, 0:B], ROWS)
        total = both[:, 0:B] + (both[:, B : 2 * B] + rest)
        wide[there] = total.reshape(4, 2, H, B)
        copies.send(("pairs", step), wide.at[there, :, 1 - core], wide_in.at[there], partner)

    def wide_ready(step):
        there = turn(x, step)
        copies.wait(("pairs", step), wide_in.at[there], partner)
        for lo in range(4):
            wide[there, lo, core] = wide[there, lo, core] + wide_in[there, lo]

    step = 2
    wide_product(turn(x, 2))
    ring[0].relay()
    step = 1
    wide_product(turn(x, 1))
    ring[1].relay()
    step = 3
    wide_product(turn(x, 3))
    ring[2].relay()

    def to_partner_half(chunk):
        quarter[chunk, 0], quarter[chunk, 1] = ring[chunk].finish()
        copies.send(("half", chunk), quarter.at[chunk], quarter_in.at[chunk], along_z(4))

    to_partner_half(0)
    step = 0
    wide_product(x)
    to_partner_half(1)
    to_partner_half(2)

    across = Scatter(
        copies, "wide", x, x_plus, x_minus,
        lambda q, h: wide.at[q, pl.ds(2 * h, 2), core],
        lambda h: wide_relay.at[h],
        lambda h: wide_direct.at[h],
        lambda h: wide_final.at[h],
    )
    wide_ready(2)
    across.start_far()
    wide_ready(1)
    across.start_plus()
    wide_ready(3)
    across.start_minus()
    wide_ready(0)

    turned_copies = []
    for step in range(1, 8):
        there = turn(row, step, 8)
        turned_copies.append(
            pltpu.make_async_remote_copy(
                src_ref=turned.at[there],
                dst_ref=turned_in,
                send_sem=send_sems.at[copies.slot(copies.sends, ("turned", step))],
                recv_sem=recv_sems.at[copies.slot(copies.recvs, "turned")],
                device_id=(there, col),
                device_id_type=MESH,
            )
        )

    @pl.when(is_owner)
    def _():
        block = pan1[pl.ds(pl.multiple_of(lax.rem(col, 4) * B, B), B), :]
        turned[...] = block.T.reshape(8, H, B)
        for copy in turned_copies:
            copy.start()
        turned_in[...] = turned[row]

    gather = []
    piece_copies = []
    for chunk in range(CH):
        gather.append(
            Gather(copies, ("gather", chunk), y, y_plus, y_minus, lambda q, h, chunk=chunk: column.at[chunk, q, h])
        )

    def give(chunk, half):
        remote = copies.make(
            ("piece", chunk), column.at[chunk, y, half], link_rows.at[chunk], taker(half), ("piece", chunk, half)
        )
        local = pltpu.make_async_copy(
            column.at[chunk, y, half],
            link_rows.at[chunk],
            recv_sems.at[copies.slot(copies.recvs, ("piece", chunk))],
        )
        here = is_self(half)
        piece_copies.append((half, remote))

        @pl.when(jnp.logical_and(gives, jnp.logical_not(here)))
        def _():
            remote.start()

        @pl.when(jnp.logical_and(gives, here))
        def _():
            local.start()

    for chunk in range(CH):
        copies.wait(("half", chunk), quarter_in.at[chunk], along_z(4))
        column[chunk, y] = quarter[chunk] + quarter_in[chunk]
        gather[chunk].start()
        give(chunk, 0)
        give(chunk, 1)

    across.relay()
    for chunk in range(CH):
        gather[chunk].relay()

    link_high[...], link_low[...] = split(link[...])
    base[...] = product(split(diag[...]), (link_high[...], link_low[...]))

    mine[0:2], mine[2:4] = across.finish()
    for step in range(1, 4):
        there = turn(zl, step)
        copies.send(("line", step), mine.at[there], mine_in.at[step - 1], device(zl=there))

    for chunk in range(CH):
        gather[chunk].near()
        gather[chunk].far()
        column_first[:, chunk * W : (chunk + 1) * W] = column[chunk].reshape(B, W)

    @pl.when(jnp.logical_not(is_owner))
    def _():
        turned_copies[0].wait_recv()

    whole = split(column_first[...])
    slice_first = product(split(turned_in[...]), whole)
    both = mul(whole[0], pan2_cat[...], ROWS)
    rest = mul(whole[1], pan2_cat[:, 0:B], ROWS)
    cross[...] = both[:, 0:B] + (both[:, B : 2 * B] + rest)
    pair[0] = slice_first.reshape(3, S, B)
    slice_second = cross[pl.ds(pl.multiple_of(row * H, H), H), :] - product(
        split(slice_first), (link_high[...], link_low[...])
    )
    pair[1] = slice_second.reshape(3, S, B)
    copies.send("pair", pair.at[1 - core], pair_in, partner)
    copies.wait("pair", pair_in, partner)
    slices[...] = pair[core] + pair_in[...]
    for step, there in ((1, x_plus), (2, x_far), (3, x_minus)):
        copies.send(("slice", step), slices.at[jnp.minimum(turn(x, step), 2)], slices_in.at[step - 1], there)
    for step, there in ((1, x_minus), (2, x_far), (3, x_plus)):
        copies.wait(("slice", step), slices_in.at[step - 1], there)
    depth[z] = (slices[jnp.minimum(x, 2)] + slices_in[0]) + (slices_in[1] + slices_in[2])
    for step in range(1, 8):
        copies.send(("depth", step), depth.at[z], depth.at[z], along_z(step))

    for step in range(1, 4):
        copies.wait(("line", step), mine_in.at[step - 1], device(zl=turn(zl, 4 - step)))
    for chunk in range(CH):
        copies.wait(("piece", chunk), link_rows.at[chunk], partner)
    block_row = row * 4 + lax.div(col, 8)
    rows_here = jnp.concatenate([link_rows[chunk] for chunk in range(CH)], axis=1)
    total = (mine[zl] + mine_in[0]) + (mine_in[1] + mine_in[2])
    total = total + product(split(rows_here), (link_high[...], link_low[...]))
    column_second[...] = total * (-marks[1, block_row].astype(F32))

    for step in range(1, 8):
        copies.wait(("depth", step), depth.at[turn(z, 8 - step, 8)], along_z(8 - step))
    for half in range(2):
        grid[core, y, half, x] = ((depth[4 * half] + depth[4 * half + 1]) + depth[4 * half + 2]) + depth[4 * half + 3]
    gather_x = Gather(copies, "gather_x", x, x_plus, x_minus, lambda q, h: grid.at[core, y, h, q])
    gather_x.start()
    gather_x.relay()
    gather_x.near()
    gather_x.far()
    gather_y = Gather(copies, "gather_y", y, y_plus, y_minus, lambda q, h: grid.at[core, q, h, pl.ds(0, 3)])
    gather_y.start()

    def pass_on(step):
        there = turn(y, step)
        copies.send(("swap", step), grid.at[core, there, :, pl.ds(0, 3)], grid.at[core, there, :, pl.ds(0, 3)], partner)

    pass_on(0)
    gather_y.relay()
    gather_y.near()
    pass_on(3)
    pass_on(1)
    gather_y.far()
    pass_on(2)
    for step in (0, 3, 1, 2):
        there = turn(y, step)
        copies.wait(("swap", step), grid.at[1 - core, there, :, pl.ds(0, 3)], partner)
    for high_z in range(2):
        for y_at in range(4):
            at = pl.ds((high_z * 4 + y_at) * H, H)
            diag_first[at, :] = diag[at, :] - grid[0, y_at, high_z, 0:3].reshape(H, B)
            corner[at, :] = -(base[at, :] + grid[1, y_at, high_z, 0:3].reshape(H, B))

    copies.finish()
    for half, copy in piece_copies:

        @pl.when(jnp.logical_and(gives, jnp.logical_not(is_self(half))))
        def _(copy=copy):
            copy.wait_send()

    @pl.when(is_owner)
    def _():
        for copy in turned_copies:
            copy.wait_send()


def body(inverse_blocks, panel_first, panel_second, panel_link, diag_inverse, ancestors):
    vmem = pl.BlockSpec(memory_space=pltpu.VMEM)
    shape = jax.ShapeDtypeStruct
    return pl.pallas_call(
        kernel,
        out_shape=(shape((B, B), F32), shape((B, B), F32), shape((H, B), F32), shape((B, B), F32)),
        in_specs=[pl.BlockSpec(memory_space=pltpu.SMEM)] + [vmem] * 5,
        out_specs=(vmem,) * 4,
        scratch_shapes=[
            pltpu.VMEM((B, 4 * B), BF16),
            pltpu.VMEM((B, 4 * B), BF16),
            pltpu.VMEM((CH, 4 * B, 2 * W), BF16),
            pltpu.VMEM((B, 2 * B), BF16),
            pltpu.VMEM((B, B), BF16),
            pltpu.VMEM((B, B), BF16),
            pltpu.VMEM((B, B), F32),
            pltpu.VMEM((CH, 4, 2, H, W), F32),
            pltpu.VMEM((CH, 2, H, W), F32),
            pltpu.VMEM((CH, 2, H, W), F32),
            pltpu.VMEM((CH, 2, H, W), F32),
            pltpu.VMEM((CH, 2, H, W), F32),
            pltpu.VMEM((CH, 2, H, W), F32),
            pltpu.VMEM((CH, 4, 2, H, W), F32),
            pltpu.VMEM((4, 4, 2, H, B), F32),
            pltpu.VMEM((4, 4, H, B), F32),
            pltpu.VMEM((2, 2, H, B), F32),
            pltpu.VMEM((2, 2, H, B), F32),
            pltpu.VMEM((2, 2, H, B), F32),
            pltpu.VMEM((4, H, B), F32),
            pltpu.VMEM((3, H, B), F32),
            pltpu.VMEM((CH, H, W), F32),
            pltpu.VMEM((8, H, B), F32),
            pltpu.VMEM((H, B), F32),
            pltpu.VMEM((B, B), F32),
            pltpu.VMEM((2, 3, S, B), F32),
            pltpu.VMEM((3, S, B), F32),
            pltpu.VMEM((3, S, B), F32),
            pltpu.VMEM((3, S, B), F32),
            pltpu.VMEM((8, S, B), F32),
            pltpu.VMEM((2, 4, 2, 4, S, B), F32),
            pltpu.SemaphoreType.DMA((112,)),
            pltpu.SemaphoreType.DMA((112,)),
        ],
        compiler_params=pltpu.CompilerParams(
            collective_id=0, has_side_effects=True, vmem_limit_bytes=60 * 1024 * 1024
        ),
    )(ancestors, inverse_blocks, panel_first, panel_second, panel_link, diag_inverse)


def solution(mesh):
    placed = (P("pcol", "prow"), P("prow", None), P("pcol", None), P(), P(), P())
    return jax.shard_map(
        body,
        mesh=mesh,
        in_specs=placed,
        out_specs=(P("pcol", None), P(), P(("prow", "pcol"), None), P()),
        check_vma=False,
    )
```

time: 580 us -> 79.8 us (0.14)
  waiting for transfers between devices: 522 us -> 0 us
  Pallas kernels: 0 us -> 73.6 us
  matrix products: 26.3 us -> 0 us
  between operations: 14.5 us -> 0.66 us
    psum x2 -> x0, waiting for transfers between devices: 378 us -> none  [the longest x1 265 us: body(): diag_first = diag_inverse - lax.psum(block_coupling, 'pcol')]
    unnamed x4 -> x0, waiting for transfers between devices: 144 us -> none
    pallas_call x0 -> x1, Pallas kernels: none -> 73.6 us  [body(): pl.pallas_call(kernel, out_shape=(shape((B, B), F32), shape((B, B), F32),...]
    dot_general x6 -> x0, matrix products: 26.3 us -> none  [the longest x3 15.8 us: product(): jnp.dot(left, right, precision=lax.Precision.HIGHEST, preferred_element_t...]
  transfers between devices with their start and end apart: 3 -> 0, of which waited for: 3 -> 0; matrix products, arithmetic and copies ran while one was open for 3% -> 0% of each run, Pallas kernels for 0% -> 0%
where the time goes in v1:
time: 79.8 us; the launch traced here: 79.6 us
  Pallas kernels  73.6 us (92%)
  local copies, waits for them, and re-layouts  5.35 us (7%)
    pallas_call x1, Pallas kernels, body(): pl.pallas_call(kernel, out_shape=(shape((B, B), F32), shape((B, B), F32),...  73.6 us
    unnamed x8, local copies, waits for them, and re-layouts  5.35 us

profile of v1, /device:TPU:1, one launch (start us, length us, event | category | flops | bytes accessed | tf_op | source)
XLA Modules:
  0.0 79.6 jit_solution(12086886278490641432)
XLA Ops:
  0.6 73.6 %shard_map.93 = (f32[384,384]{1,0:T(8,128)}, f32[384,384]{1,0:T(8,128)}, f32[48,384]{1,0:T(8,128)}, f32[384,384]{1,0:T(8,128)}) custom-call(s32[2,32]{1,0:T(2,128)} %marks.1, f32[384,1536]{1,0:T(8,128)} %inv.1, f32[1536,384]{1,0:T(8,128)} %pan1.1, f32[384,384]{1,0:T(8,128)} %pan2.1, f32[384,384]{1,0:T(8,128)} %link.1, f32[384,384]{1,0:T(8,128)} %diag.1), custom_call_target="tpu_custom_call" | custom-call | tf_op jit(solution)/shard_map/pallas_call | solution.py:452
  74.3 0.0 copy-start.1
  74.3 0.0 copy-start
  74.3 2.0 %copy.14 = f32[384,384]{1,0:T(8,128)} copy(f32[384,384]{1,0:T(8,128)} %get-tuple-element.8) | data formatting | bytes 1179648
  76.3 1.9 %copy.15 = f32[384,384]{1,0:T(8,128)} copy(f32[384,384]{1,0:T(8,128)} %get-tuple-element.9) | data formatting | bytes 1179648
  78.2 0.0 copy-done.1
  78.2 0.6 copy.16
  78.8 0.0 copy-done
  78.8 0.8 %copy.17 = f32[384,384]{1,0:T(8,128)} copy(f32[384,384]{1,0:T(8,128)S(1)} %copy-done) | data formatting | bytes 1179648
Async XLA Ops:
  74.3 3.9 %copy-start.1 = (f32[48,384]{1,0:T(8,128)S(1)}, f32[48,384]{1,0:T(8,128)}, u32[]{:S(2)}) copy-start(f32[48,384]{1,0:T(8,128)} %get-tuple-element.10) | copy-start | bytes 221188
  74.3 4.5 %copy-start = (f32[384,384]{1,0:T(8,128)S(1)}, f32[384,384]{1,0:T(8,128)}, u32[]{:S(2)}) copy-start(f32[384,384]{1,0:T(8,128)} %get-tuple-element.11) | copy-start | bytes 1769476

commit v2 on v1

--- a/solution.py
+++ b/solution.py
@@ -134,8 +134,8 @@
 
 
 def kernel(
-    marks, inv, pan1, pan2, link, diag, column_first, diag_first, column_second, corner,
-    inv_high, inv_low, pan1_cat, pan2_cat, link_high, link_low, base,
+    marks, inv_hbm, pan1_hbm, pan2_hbm, link_hbm, diag_hbm, column_first, diag_first, column_second, corner,
+    inv, pan1, pan2, link, diag, load_sems, inv_high, inv_low, pan1_cat, pan2_cat, link_high, link_low, base,
     part, part_relay, part_direct, part_final, quarter, quarter_in, column,
     wide, wide_in, wide_relay, wide_direct, wide_final, mine, mine_in, link_rows,
     turned, turned_in, cross, pair, pair_in, slices, slices_in, depth, grid,
@@ -156,11 +156,22 @@
         there = turn(z, step, 8)
         return device(zh=lax.div(there, 4), zl=lax.rem(there, 4))
 
+    loads = []
+    for block in range(4):
+        at = pl.ds(block * B, B)
+        loads.append((pan1_hbm.at[at, :], pan1.at[at, :]))
+        loads.append((inv_hbm.at[:, at], inv.at[:, at]))
+    loads += [(pan2_hbm, pan2), (link_hbm, link), (diag_hbm, diag)]
+    loads = [pltpu.make_async_copy(src, dst, load_sems.at[at]) for at, (src, dst) in enumerate(loads)]
+
     y_plus, y_minus = device(y=turn(y, 1)), device(y=turn(y, 3))
     x_plus, x_minus, x_far = device(x=turn(x, 1)), device(x=turn(x, 3)), device(x=turn(x, 2))
     partner = device(core=1 - core)
     owner_row = lax.div(col, 4)
     is_owner = row == owner_row
+    owner_y, owner_zh = lax.rem(owner_row, 4), lax.div(owner_row, 4)
+    is_source = y == owner_y
+    is_deputy = jnp.logical_and(is_source, zh != owner_zh)
 
     gives = zh == lax.div(col, 16)
 
@@ -188,9 +199,12 @@
     def _():
         greet(giver)
 
-    @pl.when(jnp.logical_not(is_owner))
-    def _():
-        greet((owner_row, col))
+    @pl.when(jnp.logical_not(is_source))
+    def _():
+        greet(device(y=owner_y))
+
+    for load in loads:
+        load.start()
 
     copies = Copies(send_sems, recv_sems)
 
@@ -198,6 +212,8 @@
     second_own = marks[1, col].astype(F32)
     for block in range(4):
         at = pl.ds(block * B, B)
+        loads[2 * block].wait()
+        loads[2 * block + 1].wait()
         scaled = pan1[at, :] * marks[0, row * 4 + block].astype(F32)
         high, low = split(scaled)
         for chunk in range(CH):
@@ -230,7 +246,7 @@
         ring[chunk].start_minus()
 
     partial_product(0)
-    waits = 13 + jnp.where(is_owner, 7, 0)
+    waits = 13 + jnp.where(is_source, 3, 0)
     for half in range(2):
         waits = waits + jnp.where(jnp.logical_and(gives, jnp.logical_not(is_self(half))), 1, 0)
     pl.semaphore_wait(barrier, waits)
@@ -240,6 +256,28 @@
     partial_product(2)
     start_ring(2)
 
+    turned_copies = []
+    for step in range(1, 4):
+        turned_copies.append(
+            copies.make(
+                "turned", turned.at[zh * 4 + turn(y, step)], turned_in, device(y=turn(y, step)), ("turned", step)
+            )
+        )
+    far = turned.at[pl.ds(4 * (1 - zh), 4)]
+    turned_far = copies.make("turned_far", far, far, along_z(4))
+
+    def turned_out():
+        for copy in turned_copies:
+            copy.start()
+        turned_in[...] = turned[row]
+
+    @pl.when(is_owner)
+    def _():
+        block = pan1[pl.ds(pl.multiple_of(lax.rem(col, 4) * B, B), B), :]
+        turned[...] = block.T.reshape(8, H, B)
+        turned_far.start()
+
+    loads[8].wait()
     high, low = split(pan2[...] * second_own)
     pan2_cat[:, 0:B] = high
     pan2_cat[:, B : 2 * B] = low
@@ -267,6 +305,10 @@
     step = 3
     wide_product(turn(x, 3))
     ring[2].relay()
+
+    @pl.when(is_owner)
+    def _():
+        turned_out()
 
     def to_partner_half(chunk):
         quarter[chunk, 0], quarter[chunk, 1] = ring[chunk].finish()
@@ -293,28 +335,6 @@
     across.start_minus()
     wide_ready(0)
 
-    turned_copies = []
-    for step in range(1, 8):
-        there = turn(row, step, 8)
-        turned_copies.append(
-            pltpu.make_async_remote_copy(
-                src_ref=turned.at[there],
-                dst_ref=turned_in,
-                send_sem=send_sems.at[copies.slot(copies.sends, ("turned", step))],
-                recv_sem=recv_sems.at[copies.slot(copies.recvs, "turned")],
-                device_id=(there, col),
-                device_id_type=MESH,
-            )
-        )
-
-    @pl.when(is_owner)
-    def _():
-        block = pan1[pl.ds(pl.multiple_of(lax.rem(col, 4) * B, B), B), :]
-        turned[...] = block.T.reshape(8, H, B)
-        for copy in turned_copies:
-            copy.start()
-        turned_in[...] = turned[row]
-
     gather = []
     piece_copies = []
     for chunk in range(CH):
@@ -346,27 +366,30 @@
         copies.wait(("half", chunk), quarter_in.at[chunk], along_z(4))
         column[chunk, y] = quarter[chunk] + quarter_in[chunk]
         gather[chunk].start()
+
+    @pl.when(is_deputy)
+    def _():
+        turned_far.wait_recv()
+        turned_out()
+
+    for chunk in range(CH):
+        gather[chunk].relay()
         give(chunk, 0)
         give(chunk, 1)
-
     across.relay()
-    for chunk in range(CH):
-        gather[chunk].relay()
+
+    loads[9].wait()
+    loads[10].wait()
 
     link_high[...], link_low[...] = split(link[...])
     base[...] = product(split(diag[...]), (link_high[...], link_low[...]))
-
-    mine[0:2], mine[2:4] = across.finish()
-    for step in range(1, 4):
-        there = turn(zl, step)
-        copies.send(("line", step), mine.at[there], mine_in.at[step - 1], device(zl=there))
 
     for chunk in range(CH):
         gather[chunk].near()
         gather[chunk].far()
         column_first[:, chunk * W : (chunk + 1) * W] = column[chunk].reshape(B, W)
 
-    @pl.when(jnp.logical_not(is_owner))
+    @pl.when(jnp.logical_not(is_source))
     def _():
         turned_copies[0].wait_recv()
 
@@ -391,15 +414,10 @@
     for step in range(1, 8):
         copies.send(("depth", step), depth.at[z], depth.at[z], along_z(step))
 
+    mine[0:2], mine[2:4] = across.finish()
     for step in range(1, 4):
-        copies.wait(("line", step), mine_in.at[step - 1], device(zl=turn(zl, 4 - step)))
-    for chunk in range(CH):
-        copies.wait(("piece", chunk), link_rows.at[chunk], partner)
-    block_row = row * 4 + lax.div(col, 8)
-    rows_here = jnp.concatenate([link_rows[chunk] for chunk in range(CH)], axis=1)
-    total = (mine[zl] + mine_in[0]) + (mine_in[1] + mine_in[2])
-    total = total + product(split(rows_here), (link_high[...], link_low[...]))
-    column_second[...] = total * (-marks[1, block_row].astype(F32))
+        there = turn(zl, step)
+        copies.send(("line", step), mine.at[there], mine_in.at[step - 1], device(zl=there))
 
     for step in range(1, 8):
         copies.wait(("depth", step), depth.at[turn(z, 8 - step, 8)], along_z(8 - step))
@@ -424,6 +442,16 @@
     pass_on(1)
     gather_y.far()
     pass_on(2)
+    for step in range(1, 4):
+        copies.wait(("line", step), mine_in.at[step - 1], device(zl=turn(zl, 4 - step)))
+    for chunk in range(CH):
+        copies.wait(("piece", chunk), link_rows.at[chunk], partner)
+    block_row = row * 4 + lax.div(col, 8)
+    rows_here = jnp.concatenate([link_rows[chunk] for chunk in range(CH)], axis=1)
+    total = (mine[zl] + mine_in[0]) + (mine_in[1] + mine_in[2])
+    total = total + product(split(rows_here), (link_high[...], link_low[...]))
+    column_second[...] = total * (-marks[1, block_row].astype(F32))
+
     for step in (0, 3, 1, 2):
         there = turn(y, step)
         copies.wait(("swap", step), grid.at[1 - core, there, :, pl.ds(0, 3)], partner)
@@ -440,21 +468,43 @@
         def _(copy=copy):
             copy.wait_send()
 
-    @pl.when(is_owner)
+    @pl.when(is_source)
     def _():
         for copy in turned_copies:
             copy.wait_send()
 
-
-def body(inverse_blocks, panel_first, panel_second, panel_link, diag_inverse, ancestors):
+    @pl.when(is_owner)
+    def _():
+        turned_far.wait_send()
+
+
+def deliver(*refs):
+    sems = refs[-1]
+    moves = [pltpu.make_async_copy(refs[at], refs[4 + at], sems.at[at]) for at in range(4)]
+    for move in moves:
+        move.start()
+    for move in moves:
+        move.wait()
+
+
+def body(*arrays):
+    *arrays, ancestors = arrays
     vmem = pl.BlockSpec(memory_space=pltpu.VMEM)
+    hbm = pl.BlockSpec(memory_space=pltpu.HBM)
     shape = jax.ShapeDtypeStruct
-    return pl.pallas_call(
+    sizes = ((B, B), (B, B), (H, B), (B, B))
+    held = pl.pallas_call(
         kernel,
-        out_shape=(shape((B, B), F32), shape((B, B), F32), shape((H, B), F32), shape((B, B), F32)),
-        in_specs=[pl.BlockSpec(memory_space=pltpu.SMEM)] + [vmem] * 5,
+        out_shape=tuple(pltpu.VMEM(size, F32) for size in sizes),
+        in_specs=[pl.BlockSpec(memory_space=pltpu.SMEM)] + [hbm] * 5,
         out_specs=(vmem,) * 4,
         scratch_shapes=[
+            pltpu.VMEM((B, 4 * B), F32),
+            pltpu.VMEM((4 * B, B), F32),
+            pltpu.VMEM((B, B), F32),
+            pltpu.VMEM((B, B), F32),
+            pltpu.VMEM((B, B), F32),
+            pltpu.SemaphoreType.DMA((11,)),
             pltpu.VMEM((B, 4 * B), BF16),
             pltpu.VMEM((B, 4 * B), BF16),
             pltpu.VMEM((CH, 4 * B, 2 * W), BF16),
@@ -490,9 +540,17 @@
             pltpu.SemaphoreType.DMA((112,)),
         ],
         compiler_params=pltpu.CompilerParams(
-            collective_id=0, has_side_effects=True, vmem_limit_bytes=60 * 1024 * 1024
+            collective_id=0, has_side_effects=True, vmem_limit_bytes=44 * 1024 * 1024
         ),
-    )(ancestors, inverse_blocks, panel_first, panel_second, panel_link, diag_inverse)
+    )(ancestors, *[pltpu.with_memory_space_constraint(given, pltpu.HBM) for given in arrays])
+    held = [pltpu.with_memory_space_constraint(made, pltpu.VMEM) for made in held]
+    return pl.pallas_call(
+        deliver,
+        out_shape=tuple(shape(size, F32) for size in sizes),
+        in_specs=[vmem] * 4,
+        out_specs=(hbm,) * 4,
+        scratch_shapes=[pltpu.SemaphoreType.DMA((4,))],
+    )(*held)
 
 
 def solution(mesh):

time: 79.8 us -> 70.1 us (0.88)
  Pallas kernels: 73.6 us -> 68.7 us
  local copies, waits for them, and re-layouts: 5.35 us -> 0.67 us
    pallas_call x1 -> x2, Pallas kernels: 73.6 us -> 68.7 us  [the longest x1 67.5 us: body(): pl.pallas_call(kernel, out_shape=tuple((pltpu.VMEM(size, F32) for size in...]
    unnamed x8 -> x2, local copies, waits for them, and re-layouts: 5.35 us -> 0.67 us
where the time goes in v2:
time: 70.1 us
  Pallas kernels  68.7 us (98%)
    pallas_call x1, Pallas kernels, body(): pl.pallas_call(kernel, out_shape=tuple((pltpu.VMEM(size, F32) for size in...  67.5 us

profile of v2, /device:TPU:1, one launch (start us, length us, event | category | flops | bytes accessed | tf_op | source)
XLA Modules:
  0.0 70.1 jit_solution(7855860937395700194)
XLA Ops:
  0.6 0.0 copy-start
  0.6 0.7 copy-done
  1.3 67.5 %shard_map.93 = (f32[384,384]{1,0:T(8,128)S(1)}, f32[384,384]{1,0:T(8,128)S(1)}, f32[48,384]{1,0:T(8,128)S(1)}, f32[384,384]{1,0:T(8,128)S(1)}) custom-call(s32[2,32]{1,0:T(2,128)S(1)} %copy-done, f32[384,1536]{1,0:T(8,128)} %inv_hbm.1, f32[1536,384]{1,0:T(8,128)} %pan1_hbm.1, f32[384,384]{1,0:T(8,128)} %pan2_hbm.1, f32[384,384]{1,0:T(8,128)} %link_hbm.1, ...), custom_call_target="tpu_custom_call" | custom-call | tf_op jit(solution)/shard_map/pallas_call | solution.py:496
  68.8 1.3 %shard_map.94 = (f32[384,384]{1,0:T(8,128)}, f32[384,384]{1,0:T(8,128)}, f32[48,384]{1,0:T(8,128)}, f32[384,384]{1,0:T(8,128)}) custom-call(f32[384,384]{1,0:T(8,128)S(1)} %get-tuple-element.8.refs_0_, f32[384,384]{1,0:T(8,128)S(1)} %get-tuple-element.9.refs_1_, f32[48,384]{1,0:T(8,128)S(1)} %get-tuple-element.10.refs_2_, ...), custom_call_target="tpu_custom_call" | custom-call | tf_op jit(solution)/shard_map/pallas_call | solution.py:547
Async XLA Ops:
  0.6 0.7 copy-start

commit v3 on v2

v3 whole, which is shorter than its diff:
```python
import functools

import jax
import jax.numpy as jnp
from jax import lax
from jax.experimental import pallas as pl
from jax.experimental.pallas import tpu as pltpu
from jax.sharding import PartitionSpec as P

MESH = pl.DeviceIdType.MESH
F32 = jnp.float32
BF16 = jnp.bfloat16
B = 384
CH = 3
W = 128
H = 48
Q = 96
S = 16
ROWS = (((0,), (0,)), ((), ()))
PLAIN = (((1,), (0,)), ((), ()))


def split(value):
    high = value.astype(BF16)
    low = (value - high.astype(F32)).astype(BF16)
    return high, low


def mul(left, right, dims=PLAIN):
    return lax.dot_general(left, right, dims, preferred_element_type=F32)


def product(left, right, dims=PLAIN):
    left_high, left_low = left
    right_high, right_low = right
    return mul(left_high, right_high, dims) + (mul(left_high, right_low, dims) + mul(left_low, right_high, dims))


class Copies:
    def __init__(self, send_sems, recv_sems):
        self.send_sems, self.recv_sems = send_sems, recv_sems
        self.sends, self.recvs, self.sent = {}, {}, []

    def slot(self, table, key):
        if key not in table:
            table[key] = len(table)
        return table[key]

    def make(self, key, src, dst, device, send_key=None):
        send = self.slot(self.sends, key if send_key is None else send_key)
        recv = self.slot(self.recvs, key)
        return pltpu.make_async_remote_copy(
            src_ref=src,
            dst_ref=dst,
            send_sem=self.send_sems.at[send],
            recv_sem=self.recv_sems.at[recv],
            device_id=device,
            device_id_type=MESH,
        )

    def send(self, key, src, dst, device):
        copy = self.make(key, src, dst, device)
        copy.start()
        self.sent.append(copy)

    def wait(self, key, dst, device):
        self.make(key, dst, dst, device).wait_recv()

    def finish(self):
        for copy in self.sent:
            copy.wait_send()


class Exchange:
    def __init__(self, copies, name, pos, size, device, src, dst, land):
        self.copies, self.name, self.pos, self.size, self.device = copies, name, pos, size, device
        self.src, self.dst, self.land = src, dst, land
        self.steps = [2, 1, 3] if size == 4 else [4, 3, 5, 2, 6, 1, 7]

    def at(self, step):
        return lax.rem(self.pos + step, self.size)

    def start(self):
        for step in self.steps:
            there = self.at(step)
            self.copies.send((self.name, step), self.src(there), self.dst(step), self.device(there))

    def wait(self, step):
        back = self.at(self.size - step)
        self.copies.wait((self.name, step), self.land(step, back), self.device(back))

    def finish(self):
        for step in reversed(self.steps):
            self.wait(step)


def kernel(
    marks, inv_hbm, pan1_hbm, pan2_hbm, link_hbm, diag_hbm, column_first, diag_first, column_second, corner,
    inv, pan1, pan2, link, diag, load_sems, inv_high, inv_low, pan1_cat, pan2_cat, link_high, link_low,
    part, part_in, quarter, quarter_in, column,
    wide, wide_in, wide_far, mine, mine_in, link_rows,
    turned, turned_in, cross, pair, pair_in, slices, slices_in, depth, grid,
    send_sems, recv_sems,
):
    row, col = lax.axis_index("prow"), lax.axis_index("pcol")
    y, zh = lax.rem(row, 4), lax.div(row, 4)
    x, zl, core = lax.div(col, 8), lax.rem(lax.div(col, 2), 4), lax.rem(col, 2)
    z = zh * 4 + zl

    def device(y=y, zh=zh, x=x, zl=zl, core=core):
        return (zh * 4 + y, (x * 4 + zl) * 2 + core)

    def turn(value, step, size=4):
        return lax.rem(value + step, size)

    def at_z(there):
        return device(zh=lax.div(there, 4), zl=lax.rem(there, 4))

    def at_y(there):
        return device(y=there)

    def at_x(there):
        return device(x=there)

    loads = []
    for block in range(4):
        at = pl.ds(block * B, B)
        loads.append((pan1_hbm.at[at, :], pan1.at[at, :]))
        loads.append((inv_hbm.at[:, at], inv.at[:, at]))
    loads += [(pan2_hbm, pan2), (link_hbm, link), (diag_hbm, diag)]
    loads = [pltpu.make_async_copy(src, dst, load_sems.at[at]) for at, (src, dst) in enumerate(loads)]

    partner = device(core=1 - core)
    opposite = at_z(turn(z, 4, 8))
    owner_row = lax.div(col, 4)
    is_owner = row == owner_row
    owner_y, owner_zh = lax.rem(owner_row, 4), lax.div(owner_row, 4)
    is_source = y == owner_y
    is_deputy = jnp.logical_and(is_source, zh != owner_zh)

    gives = zh == lax.div(col, 16)

    def taker(half):
        return (owner_row, lax.rem(col, 4) * 8 + y * 2 + half)

    def is_self(half):
        there = taker(half)
        return jnp.logical_and(there[0] == row, there[1] == col)

    giver = (zh * 4 + lax.div(lax.rem(col, 8), 2), row * 4 + lax.div(col, 8))
    from_self = jnp.logical_and(giver[0] == row, giver[1] == col)

    barrier = pltpu.get_barrier_semaphore()

    def greet(there):
        pl.semaphore_signal(barrier, inc=1, device_id=there, device_id_type=MESH)

    for step in (1, 2, 3):
        greet(at_y(turn(y, step)))
        greet(at_x(turn(x, step)))
    greet(partner)
    for step in range(1, 8):
        greet(at_z(turn(z, step, 8)))

    @pl.when(jnp.logical_not(from_self))
    def _():
        greet(giver)

    @pl.when(jnp.logical_not(is_source))
    def _():
        greet(device(y=owner_y))

    for load in loads:
        load.start()

    copies = Copies(send_sems, recv_sems)

    first_own = marks[0, col].astype(F32)
    second_own = marks[1, col].astype(F32)
    for block in range(4):
        at = pl.ds(block * B, B)
        loads[2 * block].wait()
        scaled = pan1[at, :] * marks[0, row * 4 + block].astype(F32)
        high, low = split(scaled)
        for chunk in range(CH):
            lanes = slice(chunk * W, (chunk + 1) * W)
            pan1_cat[chunk, at, 0:W] = high[:, lanes]
            pan1_cat[chunk, at, W : 2 * W] = low[:, lanes]
        loads[2 * block + 1].wait()
        inv_high[:, at], inv_low[:, at] = split(inv[:, at])

    def partial_product(chunk):
        both = mul(inv_high[...], pan1_cat[chunk])
        rest = mul(inv_low[...], pan1_cat[chunk, :, 0:W])
        total = (both[:, 0:W] + (both[:, W : 2 * W] + rest)) * (-first_own)
        part[chunk] = total.reshape(4, Q, W)

    scatter, gather, along_x, along_z, gather_x, gather_y = [], [], [], [], [], []
    for chunk in range(CH):
        scatter.append(
            Exchange(
                copies, ("part", chunk), y, 4, at_y,
                lambda there, k=chunk: part.at[k, there],
                lambda step, k=chunk: part_in.at[k, step - 1],
                lambda step, back, k=chunk: part_in.at[k, step - 1],
            )
        )
        gather.append(
            Exchange(
                copies, ("column", chunk), y, 4, at_y,
                lambda there, k=chunk: column.at[k, y],
                lambda step, k=chunk: column.at[k, y],
                lambda step, back, k=chunk: column.at[k, back],
            )
        )
        along_x.append(
            Exchange(
                copies, ("slices", chunk), x, 4, at_x,
                lambda there, k=chunk: slices.at[k, jnp.minimum(there, 2)],
                lambda step, k=chunk: slices_in.at[k, step - 1],
                lambda step, back, k=chunk: slices_in.at[k, step - 1],
            )
        )
        along_z.append(
            Exchange(
                copies, ("depth", chunk), z, 8, at_z,
                lambda there, k=chunk: depth.at[k, z],
                lambda step, k=chunk: depth.at[k, z],
                lambda step, back, k=chunk: depth.at[k, back],
            )
        )
        gather_x.append(
            Exchange(
                copies, ("grid_x", chunk), x, 4, at_x,
                lambda there, k=chunk: grid.at[k, core, y, :, x],
                lambda step, k=chunk: grid.at[k, core, y, :, x],
                lambda step, back, k=chunk: grid.at[k, core, y, :, back],
            )
        )
        gather_y.append(
            Exchange(
                copies, ("grid_y", chunk), y, 4, at_y,
                lambda there, k=chunk: grid.at[k, core, y, :, pl.ds(0, 3)],
                lambda step, k=chunk: grid.at[k, core, y, :, pl.ds(0, 3)],
                lambda step, back, k=chunk: grid.at[k, core, back, :, pl.ds(0, 3)],
            )
        )
    across = Exchange(
        copies, "wide", x, 4, at_x,
        lambda there: wide.at[there, :, core],
        lambda step: wide_far.at[step - 1],
        lambda step, back: wide_far.at[step - 1],
    )
    line = Exchange(
        copies, "line", zl, 4, lambda there: device(zl=there),
        lambda there: mine.at[there],
        lambda step: mine_in.at[step - 1],
        lambda step, back: mine_in.at[step - 1],
    )

    turned_copies = []
    for step in range(1, 4):
        turned_copies.append(
            copies.make(
                "turned", turned.at[zh * 4 + turn(y, step)], turned_in, at_y(turn(y, step)), ("turned", step)
            )
        )
    far = turned.at[pl.ds(4 * (1 - zh), 4)]
    turned_far = copies.make("turned_far", far, far, opposite)

    def turned_out():
        for copy in turned_copies:
            copy.start()
        turned_in[...] = turned[row]

    partial_product(0)

    @pl.when(is_owner)
    def _():
        block = pan1[pl.ds(pl.multiple_of(lax.rem(col, 4) * B, B), B), :]
        turned[...] = block.T.reshape(8, H, B)

    waits = 14 + jnp.where(is_source, 3, 0)
    for half in range(2):
        waits = waits + jnp.where(jnp.logical_and(gives, jnp.logical_not(is_self(half))), 1, 0)
    pl.semaphore_wait(barrier, waits)
    scatter[0].start()

    @pl.when(is_owner)
    def _():
        turned_far.start()

    partial_product(1)
    scatter[1].start()
    partial_product(2)
    scatter[2].start()

    loads[8].wait()
    high, low = split(pan2[...] * second_own)
    pan2_cat[:, 0:B] = high
    pan2_cat[:, B : 2 * B] = low

    def wide_product(step):
        there = turn(x, step)
        at = pl.ds(pl.multiple_of(there * B, B), B)
        both = mul(inv_high[:, at], pan2_cat[...], ROWS)
        rest = mul(inv_low[:, at], pan2_cat[:, 0:B], ROWS)
        total = both[:, 0:B] + (both[:, B : 2 * B] + rest)
        wide[there] = total.reshape(4, 2, H, B)
        copies.send(("pairs", step), wide.at[there, :, 1 - core], wide_in.at[there], partner)

    def wide_ready(step):
        there = turn(x, step)
        copies.wait(("pairs", step), wide_in.at[there], partner)
        for lo in range(4):
            wide[there, lo, core] = wide[there, lo, core] + wide_in[there, lo]

    def to_opposite(chunk):
        scatter[chunk].finish()
        quarter[chunk] = (part[chunk, y] + part_in[chunk, 0]) + (part_in[chunk, 1] + part_in[chunk, 2])
        copies.send(("half", chunk), quarter.at[chunk], quarter_in.at[chunk], opposite)

    wide_product(2)
    wide_product(1)
    to_opposite(0)

    @pl.when(is_owner)
    def _():
        turned_out()

    wide_product(3)
    to_opposite(1)
    wide_product(0)
    to_opposite(2)
    for step in (2, 1, 3):
        wide_ready(step)
        there = turn(x, step)
        copies.send(("wide", step), wide.at[there, :, core], wide_far.at[step - 1], at_x(there))
    wide_ready(0)

    @pl.when(is_deputy)
    def _():
        turned_far.wait_recv()
        turned_out()

    loads[9].wait()
    loads[10].wait()
    link_high[...], link_low[...] = split(link[...])

    for chunk in range(CH):
        copies.wait(("half", chunk), quarter_in.at[chunk], opposite)
        column[chunk, y] = quarter[chunk] + quarter_in[chunk]
        gather[chunk].start()

    piece_copies = []

    def give(chunk, half):
        src = column.at[chunk, y, pl.ds(half * H, H)]
        remote = copies.make(("piece", chunk), src, link_rows.at[chunk], taker(half), ("piece", chunk, half))
        local = pltpu.make_async_copy(src, link_rows.at[chunk], recv_sems.at[copies.slot(copies.recvs, ("piece", chunk))])
        here = is_self(half)
        piece_copies.append((half, remote))

        @pl.when(jnp.logical_and(gives, jnp.logical_not(here)))
        def _():
            remote.start()

        @pl.when(jnp.logical_and(gives, here))
        def _():
            local.start()

    for chunk in range(CH):
        give(chunk, 0)
        give(chunk, 1)

    @pl.when(jnp.logical_not(is_source))
    def _():
        turned_copies[0].wait_recv()

    turned_high, turned_low = split(turned_in[...])

    for chunk in range(CH):
        gather[chunk].finish()
        whole = column[chunk].reshape(B, W)
        column_first[:, chunk * W : (chunk + 1) * W] = whole
        whole = split(whole)
        slice_first = product((turned_high, turned_low), whole)
        both = mul(whole[0], pan2_cat[...], ROWS)
        rest = mul(whole[1], pan2_cat[:, 0:B], ROWS)
        cross[...] = both[:, 0:B] + (both[:, B : 2 * B] + rest)
        pair[chunk, 0] = slice_first.reshape(3, S, W)
        for third in range(3):
            pair[chunk, 1, third] = cross[pl.ds(pl.multiple_of(row * S, S), S), third * W : (third + 1) * W]
        copies.send(("pair", chunk), pair.at[chunk, 1 - core], pair_in.at[chunk], partner)
    for chunk in range(CH):
        copies.wait(("pair", chunk), pair_in.at[chunk], partner)
        slices[chunk] = pair[chunk, core] + pair_in[chunk]
        along_x[chunk].start()
    for chunk in range(CH):
        along_x[chunk].finish()
        depth[chunk, z] = (slices[chunk, jnp.minimum(x, 2)] + slices_in[chunk, 0]) + (
            slices_in[chunk, 1] + slices_in[chunk, 2]
        )
        along_z[chunk].start()

    across.finish()
    mine[...] = (wide[x, :, core] + wide_far[0]) + (wide_far[1] + wide_far[2])
    line.start()

    for chunk in range(CH):
        along_z[chunk].finish()
        for half in range(2):
            grid[chunk, core, y, half, x] = (
                (depth[chunk, 4 * half] + depth[chunk, 4 * half + 1]) + depth[chunk, 4 * half + 2]
            ) + depth[chunk, 4 * half + 3]
        gather_x[chunk].start()

    def pass_on(chunk, step):
        part_at = grid.at[chunk, core, turn(y, step), :, pl.ds(0, 3)]
        copies.send(("swap", chunk, step), part_at, part_at, partner)

    for chunk in range(CH):
        gather_x[chunk].finish()
        gather_y[chunk].start()
        pass_on(chunk, 0)
    for chunk in range(CH):
        for step in (1, 3, 2):
            gather_y[chunk].wait(step)
            pass_on(chunk, 4 - step)

    line.finish()
    for chunk in range(CH):
        copies.wait(("piece", chunk), link_rows.at[chunk], partner)
    block_row = row * 4 + lax.div(col, 8)
    rows_here = jnp.concatenate([link_rows[chunk] for chunk in range(CH)], axis=1)
    total = (mine[zl] + mine_in[0]) + (mine_in[1] + mine_in[2])
    total = total + product(split(rows_here), (link_high[...], link_low[...]))
    column_second[...] = total * (-marks[1, block_row].astype(F32))

    linked = []
    for chunk in range(CH):
        for step in (0, 3, 1, 2):
            part_at = grid.at[chunk, 1 - core, turn(y, step), :, pl.ds(0, 3)]
            copies.wait(("swap", chunk, step), part_at, partner)
        lanes = slice(chunk * W, (chunk + 1) * W)
        for piece in range(8):
            at = slice(piece * H, (piece + 1) * H)
            found = grid[chunk, 0, piece % 4, piece // 4, 0:3].reshape(H, W)
            diag_first[at, lanes] = diag[at, lanes] - found
        ready = split(diag_first[:, lanes])
        linked.append(product(ready, (link_high[lanes, :], link_low[lanes, :])))
    total = linked[0] + (linked[1] + linked[2])
    for chunk in range(CH):
        for piece in range(8):
            at = slice(chunk * W + piece * S, chunk * W + (piece + 1) * S)
            for third in range(3):
                lanes = slice(third * W, (third + 1) * W)
                corner[at, lanes] = -(total[at, lanes] + grid[chunk, 1, piece % 4, piece // 4, third])

    copies.finish()
    for half, copy in piece_copies:

        @pl.when(jnp.logical_and(gives, jnp.logical_not(is_self(half))))
        def _(copy=copy):
            copy.wait_send()

    @pl.when(is_source)
    def _():
        for copy in turned_copies:
            copy.wait_send()

    @pl.when(is_owner)
    def _():
        turned_far.wait_send()


def deliver(*refs):
    sems = refs[-1]
    moves = [pltpu.make_async_copy(refs[at], refs[4 + at], sems.at[at]) for at in range(4)]
    for move in moves:
        move.start()
    for move in moves:
        move.wait()


def body(*arrays):
    *arrays, ancestors = arrays
    vmem = pl.BlockSpec(memory_space=pltpu.VMEM)
    hbm = pl.BlockSpec(memory_space=pltpu.HBM)
    shape = jax.ShapeDtypeStruct
    sizes = ((B, B), (B, B), (H, B), (B, B))
    held = pl.pallas_call(
        kernel,
        out_shape=tuple(pltpu.VMEM(size, F32) for size in sizes),
        in_specs=[pl.BlockSpec(memory_space=pltpu.SMEM)] + [hbm] * 5,
        out_specs=(vmem,) * 4,
        scratch_shapes=[
            pltpu.VMEM((B, 4 * B), F32),
            pltpu.VMEM((4 * B, B), F32),
            pltpu.VMEM((B, B), F32),
            pltpu.VMEM((B, B), F32),
            pltpu.VMEM((B, B), F32),
            pltpu.SemaphoreType.DMA((11,)),
            pltpu.VMEM((B, 4 * B), BF16),
            pltpu.VMEM((B, 4 * B), BF16),
            pltpu.VMEM((CH, 4 * B, 2 * W), BF16),
            pltpu.VMEM((B, 2 * B), BF16),
            pltpu.VMEM((B, B), BF16),
            pltpu.VMEM((B, B), BF16),
            pltpu.VMEM((CH, 4, Q, W), F32),
            pltpu.VMEM((CH, 3, Q, W), F32),
            pltpu.VMEM((CH, Q, W), F32),
            pltpu.VMEM((CH, Q, W), F32),
            pltpu.VMEM((CH, 4, Q, W), F32),
            pltpu.VMEM((4, 4, 2, H, B), F32),
            pltpu.VMEM((4, 4, H, B), F32),
            pltpu.VMEM((3, 4, H, B), F32),
            pltpu.VMEM((4, H, B), F32),
            pltpu.VMEM((3, H, B), F32),
            pltpu.VMEM((CH, H, W), F32),
            pltpu.VMEM((8, H, B), F32),
            pltpu.VMEM((H, B), F32),
            pltpu.VMEM((W, B), F32),
            pltpu.VMEM((CH, 2, 3, S, W), F32),
            pltpu.VMEM((CH, 3, S, W), F32),
            pltpu.VMEM((CH, 3, S, W), F32),
            pltpu.VMEM((CH, 3, S, W), F32),
            pltpu.VMEM((CH, 8, S, W), F32),
            pltpu.VMEM((CH, 2, 4, 2, 4, S, W), F32),
            pltpu.SemaphoreType.DMA((112,)),
            pltpu.SemaphoreType.DMA((112,)),
        ],
        compiler_params=pltpu.CompilerParams(
            collective_id=0, has_side_effects=True, vmem_limit_bytes=44 * 1024 * 1024
        ),
    )(ancestors, *[pltpu.with_memory_space_constraint(given, pltpu.HBM) for given in arrays])
    held = [pltpu.with_memory_space_constraint(made, pltpu.VMEM) for made in held]
    return pl.pallas_call(
        deliver,
        out_shape=tuple(shape(size, F32) for size in sizes),
        in_specs=[vmem] * 4,
        out_specs=(hbm,) * 4,
        scratch_shapes=[pltpu.SemaphoreType.DMA((4,))],
    )(*held)


def solution(mesh):
    placed = (P("pcol", "prow"), P("prow", None), P("pcol", None), P(), P(), P())
    return jax.shard_map(
        body,
        mesh=mesh,
        in_specs=placed,
        out_specs=(P("pcol", None), P(), P(("prow", "pcol"), None), P()),
        check_vma=False,
    )
```

time: 70.1 us -> 65 us (0.927)
  Pallas kernels: 68.7 us -> 63.6 us
    pallas_call x1, Pallas kernels: 67.5 us -> 62.3 us  [body(): pl.pallas_call(kernel, out_shape=tuple((pltpu.VMEM(size, F32) for size in...]
where the time goes in v3:
time: 65 us; the launch traced here: 64.9 us
  Pallas kernels  63.6 us (98%)
  local copies, waits for them, and re-layouts  0.67 us (1%)
  between operations  0.65 us (1%)
    pallas_call x1, Pallas kernels, body(): pl.pallas_call(kernel, out_shape=tuple((pltpu.VMEM(size, F32) for size in...  62.3 us

profile of v3, /device:TPU:1, one launch (start us, length us, event | category | flops | bytes accessed | tf_op | source)
XLA Modules:
  0.0 64.9 jit_solution(9693130395281591472)
XLA Ops:
  0.6 0.0 copy-start
  0.6 0.7 %copy-done = s32[2,32]{1,0:T(2,128)S(1)} copy-done((s32[2,32]{1,0:T(2,128)S(1)}, s32[2,32]{1,0:T(2,128)}, u32[]{:S(2)}) %copy-start) | copy-done | bytes 280
  1.3 62.3 %shard_map.93 = (f32[384,384]{1,0:T(8,128)S(1)}, f32[384,384]{1,0:T(8,128)S(1)}, f32[48,384]{1,0:T(8,128)S(1)}, f32[384,384]{1,0:T(8,128)S(1)}) custom-call(s32[2,32]{1,0:T(2,128)S(1)} %copy-done, f32[384,1536]{1,0:T(8,128)} %inv_hbm.1, f32[1536,384]{1,0:T(8,128)} %pan1_hbm.1, f32[384,384]{1,0:T(8,128)} %pan2_hbm.1, f32[384,384]{1,0:T(8,128)} %link_hbm.1, ...), custom_call_target="tpu_custom_call" | custom-call | tf_op jit(solution)/shard_map/pallas_call | solution.py:492
  63.6 1.3 %shard_map.94 = (f32[384,384]{1,0:T(8,128)}, f32[384,384]{1,0:T(8,128)}, f32[48,384]{1,0:T(8,128)}, f32[384,384]{1,0:T(8,128)}) custom-call(f32[384,384]{1,0:T(8,128)S(1)} %get-tuple-element.8.refs_0_, f32[384,384]{1,0:T(8,128)S(1)} %get-tuple-element.9.refs_1_, f32[48,384]{1,0:T(8,128)S(1)} %get-tuple-element.10.refs_2_, ...), custom_call_target="tpu_custom_call" | custom-call | tf_op jit(solution)/shard_map/pallas_call | solution.py:538
Async XLA Ops:
  0.6 0.7 %copy-start = (s32[2,32]{1,0:T(2,128)S(1)}, s32[2,32]{1,0:T(2,128)}, u32[]{:S(2)}) copy-start(s32[2,32]{1,0:T(2,128)} %marks.1) | copy-start | bytes 772

commit v4 on v3

v4 whole, which is shorter than its diff:
```python
import functools

import jax
import jax.numpy as jnp
from jax import lax
from jax.experimental import pallas as pl
from jax.experimental.pallas import tpu as pltpu
from jax.sharding import PartitionSpec as P

MESH = pl.DeviceIdType.MESH
F32 = jnp.float32
BF16 = jnp.bfloat16
B = 384
CH = 3
W = 128
H = 48
S = 16
SENDS = 14
RECVS = 40
ROWS = (((0,), (0,)), ((), ()))
PLAIN = (((1,), (0,)), ((), ()))


def split(value):
    high = value.astype(BF16)
    low = (value - high.astype(F32)).astype(BF16)
    return high, low


def mul(left, right, dims=PLAIN):
    return lax.dot_general(left, right, dims, preferred_element_type=F32)


def product(left, right, dims=PLAIN):
    left_high, left_low = left
    right_high, right_low = right
    return mul(left_high, right_high, dims) + (mul(left_high, right_low, dims) + mul(left_low, right_high, dims))


class Copies:
    def __init__(self, send_sems, recv_sems):
        self.send_sems, self.recv_sems = send_sems, recv_sems
        self.kinds, self.keys = {}, {}

    def recv_sem(self, key):
        return self.recv_sems.at[self.keys.setdefault(key, len(self.keys))]

    def make(self, key, src, dst, device):
        return pltpu.make_async_remote_copy(
            src_ref=src,
            dst_ref=dst,
            send_sem=self.send_sems.at[self.kinds.setdefault(key[0], len(self.kinds))],
            recv_sem=self.recv_sem(key),
            device_id=device,
            device_id_type=MESH,
        )

    def send(self, key, src, dst, device):
        self.make(key, src, dst, device).start()

    def wait(self, key, every, device):
        self.make(key, every, every, device).wait_recv()

    def sent(self, kind, every, device):
        self.make((kind, 0), every, every, device).wait_send()


class Ring:
    def __init__(self, copies, name, pos, plus, minus, get):
        self.copies, self.name, self.pos, self.plus, self.minus, self.get = copies, name, pos, plus, minus, get

    def at(self, offset, half):
        return self.get(lax.rem(self.pos + offset, 4), half)


class Scatter(Ring):
    def __init__(self, copies, name, pos, plus, minus, get, relay, direct, final):
        super().__init__(copies, name, pos, plus, minus, get)
        self.relayed, self.direct, self.final = relay, direct, final

    def start(self):
        self.start_far()
        self.start_plus()
        self.start_minus()

    def start_far(self):
        self.copies.send((self.name, 0), self.at(2, 0), self.relayed(0), self.plus)
        self.copies.send((self.name, 1), self.at(2, 1), self.relayed(1), self.minus)

    def start_plus(self):
        self.copies.send((self.name, 2), self.at(1, 1), self.direct(0), self.plus)

    def start_minus(self):
        self.copies.send((self.name, 3), self.at(3, 0), self.direct(1), self.minus)

    def relay(self):
        self.copies.wait((self.name, 0), self.relayed(0), self.minus)
        mine = self.at(1, 0)
        mine[...] = mine[...] + self.relayed(0)[...]
        self.copies.send((self.name, 4), mine, self.final(0), self.plus)
        self.copies.wait((self.name, 1), self.relayed(1), self.plus)
        mine = self.at(3, 1)
        mine[...] = mine[...] + self.relayed(1)[...]
        self.copies.send((self.name, 5), mine, self.final(1), self.minus)

    def finish(self):
        self.copies.wait((self.name, 2), self.direct(0), self.minus)
        self.copies.wait((self.name, 3), self.direct(1), self.plus)
        self.copies.wait((self.name, 4), self.final(0), self.minus)
        self.copies.wait((self.name, 5), self.final(1), self.plus)
        first = self.at(0, 0)[...] + (self.direct(1)[...] + self.final(0)[...])
        second = self.at(0, 1)[...] + (self.direct(0)[...] + self.final(1)[...])
        return first, second


class Exchange:
    def __init__(self, copies, key, pos, size, device, src, dst, every):
        self.copies, self.key, self.pos, self.size, self.device = copies, key, pos, size, device
        self.src, self.dst, self.every = src, dst, every
        self.steps = [2, 1, 3] if size == 4 else [4, 3, 5, 2, 6, 1, 7]

    def start(self):
        for step in self.steps:
            there = lax.rem(self.pos + step, self.size)
            self.copies.send(self.key, self.src(there), self.dst(step), self.device(there))

    def finish(self):
        self.copies.wait(self.key, self.every, self.device(lax.rem(self.pos + 1, self.size)))


def kernel(
    marks_hbm, inv_hbm, pan1_hbm, pan2_hbm, link_hbm, diag_hbm, column_first, diag_first, column_second, corner,
    marks, inv, pan1, pan2, link, diag, load_sems, inv_high, inv_low, pan1_cat, pan2_cat, link_high, link_low,
    part, part_in, quarter, quarter_in, column,
    wide, wide_in, wide_relay, wide_direct, wide_final, mine, mine_in, link_rows,
    turned, turned_in, cross, pair, pair_in, slices, slices_in, depth, grid,
    send_sems, recv_sems,
):
    row, col = lax.axis_index("prow"), lax.axis_index("pcol")
    y, zh = lax.rem(row, 4), lax.div(row, 4)
    x, zl, core = lax.div(col, 8), lax.rem(lax.div(col, 2), 4), lax.rem(col, 2)
    z = zh * 4 + zl

    def device(y=y, zh=zh, x=x, zl=zl, core=core):
        return (zh * 4 + y, (x * 4 + zl) * 2 + core)

    def turn(value, step, size=4):
        return lax.rem(value + step, size)

    def at_z(there):
        return device(zh=lax.div(there, 4), zl=lax.rem(there, 4))

    def at_y(there):
        return device(y=there)

    def at_x(there):
        return device(x=there)

    y_plus, y_minus = device(y=turn(y, 1)), device(y=turn(y, 3))
    x_plus, x_minus = device(x=turn(x, 1)), device(x=turn(x, 3))

    loads = []
    for block in range(4):
        at = pl.ds(block * B, B)
        loads.append((pan1_hbm.at[at, :], pan1.at[at, :]))
        loads.append((inv_hbm.at[:, at], inv.at[:, at]))
    loads += [(pan2_hbm, pan2), (link_hbm, link), (diag_hbm, diag), (marks_hbm, marks)]
    loads = [pltpu.make_async_copy(src, dst, load_sems.at[at]) for at, (src, dst) in enumerate(loads)]

    partner = device(core=1 - core)
    opposite = at_z(turn(z, 4, 8))
    after = (lax.div(col, 4), lax.rem(col, 4) * 8 + row)
    before = (lax.rem(col, 8), row * 4 + lax.div(col, 8))
    fixed = jnp.logical_and(after[0] == row, after[1] == col)
    moved = jnp.logical_not(fixed)

    barrier = pltpu.get_barrier_semaphore()

    def greet(there):
        pl.semaphore_signal(barrier, inc=1, device_id=there, device_id_type=MESH)

    loads[11].start()
    for step in (1, 2, 3):
        greet(at_y(turn(y, step)))
        greet(at_x(turn(x, step)))
    greet(partner)
    for step in range(1, 8):
        greet(at_z(turn(z, step, 8)))

    @pl.when(moved)
    def _():
        greet(after)
        greet(before)

    for load in loads[:11]:
        load.start()

    copies = Copies(send_sems, recv_sems)

    loads[11].wait()
    first_own = marks[0, col].astype(F32)
    second_own = marks[1, col].astype(F32)
    for block in range(4):
        at = pl.ds(block * B, B)
        loads[2 * block].wait()
        scaled = pan1[at, :] * marks[0, row * 4 + block].astype(F32)
        high, low = split(scaled)
        for chunk in range(CH):
            lanes = slice(chunk * W, (chunk + 1) * W)
            pan1_cat[chunk, at, 0:W] = high[:, lanes]
            pan1_cat[chunk, at, W : 2 * W] = low[:, lanes]
        loads[2 * block + 1].wait()
        inv_high[:, at], inv_low[:, at] = split(inv[:, at])

    def partial_product(chunk):
        both = mul(inv_high[...], pan1_cat[chunk])
        rest = mul(inv_low[...], pan1_cat[chunk, :, 0:W])
        total = (both[:, 0:W] + (both[:, W : 2 * W] + rest)) * (-first_own)
        part[chunk] = total.reshape(4, 2, H, W)

    scatter, gather, along_x, along_z, gather_x, gather_y = [], [], [], [], [], []
    for chunk in range(CH):
        scatter.append(
            Exchange(
                copies, ("part", chunk), y, 4, at_y,
                lambda there, k=chunk: part.at[k, there],
                lambda step, k=chunk: part_in.at[k, step - 1],
                part_in.at[chunk],
            )
        )
        gather.append(
            Exchange(
                copies, ("column", chunk), y, 4, at_y,
                lambda there, k=chunk: column.at[k, y],
                lambda step, k=chunk: column.at[k, y],
                column.at[chunk, pl.ds(0, 3)],
            )
        )
        along_x.append(
            Exchange(
                copies, ("slices", chunk), x, 4, at_x,
                lambda there, k=chunk: slices.at[k, jnp.minimum(there, 2)],
                lambda step, k=chunk: slices_in.at[k, step - 1],
                slices_in.at[chunk],
            )
        )
        along_z.append(
            Exchange(
                copies, ("depth", chunk), z, 8, at_z,
                lambda there, k=chunk: depth.at[k, z],
                lambda step, k=chunk: depth.at[k, z],
                depth.at[chunk, pl.ds(0, 7)],
            )
        )
        gather_x.append(
            Exchange(
                copies, ("grid_x", chunk), x, 4, at_x,
                lambda there, k=chunk: grid.at[k, core, y, :, x],
                lambda step, k=chunk: grid.at[k, core, y, :, x],
                grid.at[chunk, core, pl.ds(0, 3), :, 0],
            )
        )
        gather_y.append(
            Exchange(
                copies, ("grid_y", chunk), y, 4, at_y,
                lambda there, k=chunk: grid.at[k, core, y, :, pl.ds(0, 3)],
                lambda step, k=chunk: grid.at[k, core, y, :, pl.ds(0, 3)],
                grid.at[chunk, core, pl.ds(0, 3), :, pl.ds(0, 3)],
            )
        )
    across = Scatter(
        copies, "wide", x, x_plus, x_minus,
        lambda q, h: wide.at[q, pl.ds(2 * h, 2), core],
        lambda h: wide_relay.at[h],
        lambda h: wide_direct.at[h],
        lambda h: wide_final.at[h],
    )
    line = Exchange(
        copies, ("line", 0), zl, 4, lambda there: device(zl=there),
        lambda there: mine.at[there],
        lambda step: mine_in.at[step - 1],
        mine_in,
    )

    def permute(key, src, dst, there):
        remote = copies.make(key, src, dst, there)
        local = pltpu.make_async_copy(src, dst, copies.recv_sem(key))

        @pl.when(moved)
        def _():
            remote.start()

        @pl.when(fixed)
        def _():
            local.start()

    partial_product(0)

    block = pan1[pl.ds(pl.multiple_of(lax.div(col, 8) * B, B), B), :]
    turned[...] = block.T.reshape(8, H, B)
    pl.semaphore_wait(barrier, 14 + jnp.where(moved, 2, 0))
    scatter[0].start()

    partial_product(1)
    scatter[1].start()
    partial_product(2)
    scatter[2].start()

    loads[8].wait()
    high, low = split(pan2[...] * second_own)
    pan2_cat[:, 0:B] = high
    pan2_cat[:, B : 2 * B] = low

    def wide_product(step):
        there = turn(x, step)
        at = pl.ds(pl.multiple_of(there * B, B), B)
        both = mul(inv_high[:, at], pan2_cat[...], ROWS)
        rest = mul(inv_low[:, at], pan2_cat[:, 0:B], ROWS)
        total = both[:, 0:B] + (both[:, B : 2 * B] + rest)
        wide[there] = total.reshape(4, 2, H, B)
        copies.send(("pairs", step), wide.at[there, :, 1 - core], wide_in.at[there], partner)

    def wide_ready(step):
        there = turn(x, step)
        copies.wait(("pairs", step), wide_in.at[there], partner)
        for lo in range(4):
            wide[there, lo, core] = wide[there, lo, core] + wide_in[there, lo]

    def to_opposite(chunk):
        scatter[chunk].finish()
        quarter[chunk] = (part[chunk, y] + part_in[chunk, 0]) + (part_in[chunk, 1] + part_in[chunk, 2])
        copies.send(("half", chunk), quarter.at[chunk], quarter_in.at[chunk], opposite)

    wide_product(2)
    wide_product(1)
    to_opposite(0)
    wide_product(3)
    to_opposite(1)
    wide_product(0)
    to_opposite(2)
    permute(("turned", 0), turned.at[lax.rem(col, 8)], turned_in, before)
    wide_ready(2)
    across.start_far()
    wide_ready(1)
    across.start_plus()
    wide_ready(3)
    across.start_minus()
    wide_ready(0)
    loads[9].wait()
    loads[10].wait()
    link_high[...], link_low[...] = split(link[...])
    for chunk in range(CH):
        copies.wait(("half", chunk), quarter_in.at[chunk], opposite)
        column[chunk, y] = quarter[chunk] + quarter_in[chunk]
        gather[chunk].start()

    across.relay()

    copies.wait(("turned", 0), turned_in, partner)
    turned_high, turned_low = split(turned_in[...])

    for chunk in range(CH):
        gather[chunk].finish()
        whole = column[chunk].reshape(B, W)
        column_first[:, chunk * W : (chunk + 1) * W] = whole
        whole = split(whole)
        slice_first = product((turned_high, turned_low), whole)
        both = mul(whole[0], pan2_cat[...], ROWS)
        rest = mul(whole[1], pan2_cat[:, 0:B], ROWS)
        cross[...] = both[:, 0:B] + (both[:, B : 2 * B] + rest)
        pair[chunk, 0] = slice_first.reshape(3, S, W)
        for third in range(3):
            pair[chunk, 1, third] = cross[pl.ds(pl.multiple_of(row * S, S), S), third * W : (third + 1) * W]
        copies.send(("pair", chunk), pair.at[chunk, 1 - core], pair_in.at[chunk], partner)
    for chunk in range(CH):
        copies.wait(("pair", chunk), pair_in.at[chunk], partner)
        slices[chunk] = pair[chunk, core] + pair_in[chunk]
        along_x[chunk].start()
    for chunk in range(CH):
        along_x[chunk].finish()
        depth[chunk, z] = (slices[chunk, jnp.minimum(x, 2)] + slices_in[chunk, 0]) + (
            slices_in[chunk, 1] + slices_in[chunk, 2]
        )
        along_z[chunk].start()

    permute(("rows", 0), column.at[:, lax.div(row, 2), lax.rem(row, 2)], link_rows, after)

    for chunk in range(CH):
        along_z[chunk].finish()
        for half in range(2):
            grid[chunk, core, y, half, x] = (
                (depth[chunk, 4 * half] + depth[chunk, 4 * half + 1]) + depth[chunk, 4 * half + 2]
            ) + depth[chunk, 4 * half + 3]
        gather_x[chunk].start()

    mine[0:2], mine[2:4] = across.finish()
    line.start()

    def pass_on(chunk, step):
        part_at = grid.at[chunk, core, turn(y, step), :, pl.ds(0, 3)]
        copies.send(("swap", chunk), part_at, part_at, partner)

    for chunk in range(CH):
        gather_x[chunk].finish()
        gather_y[chunk].start()
        pass_on(chunk, 0)
    for chunk in range(CH):
        gather_y[chunk].finish()
        for step in (1, 3, 2):
            pass_on(chunk, step)

    line.finish()
    copies.wait(("rows", 0), link_rows, partner)
    block_row = row * 4 + lax.div(col, 8)
    rows_here = jnp.concatenate([link_rows[chunk] for chunk in range(CH)], axis=1)
    total = (mine[zl] + mine_in[0]) + (mine_in[1] + mine_in[2])
    total = total + product(split(rows_here), (link_high[...], link_low[...]))
    column_second[...] = total * (-marks[1, block_row].astype(F32))

    linked = []
    for chunk in range(CH):
        copies.wait(("swap", chunk), grid.at[chunk, 1 - core, :, :, pl.ds(0, 3)], partner)
        lanes = slice(chunk * W, (chunk + 1) * W)
        for piece in range(8):
            at = slice(piece * H, (piece + 1) * H)
            found = grid[chunk, 0, piece % 4, piece // 4, 0:3].reshape(H, W)
            diag_first[at, lanes] = diag[at, lanes] - found
        ready = split(diag_first[:, lanes])
        linked.append(product(ready, (link_high[lanes, :], link_low[lanes, :])))
    total = linked[0] + (linked[1] + linked[2])
    for chunk in range(CH):
        for piece in range(8):
            at = slice(chunk * W + piece * S, chunk * W + (piece + 1) * S)
            for third in range(3):
                lanes = slice(third * W, (third + 1) * W)
                corner[at, lanes] = -(total[at, lanes] + grid[chunk, 1, piece % 4, piece // 4, third])

    for kind, every in (
        ("part", part.at[:, pl.ds(0, 3)]),
        ("half", quarter),
        ("column", column.at[:, pl.ds(0, 3)]),
        ("pairs", wide_in),
        ("wide", wide.at[pl.ds(0, 3), :, 0]),
        ("line", mine_in),
        ("pair", pair_in),
        ("slices", slices_in),
        ("depth", depth.at[:, pl.ds(0, 7)]),
        ("grid_x", grid.at[:, 0, pl.ds(0, 3), :, 0]),
        ("grid_y", grid.at[:, 0, pl.ds(0, 3), :, pl.ds(0, 3)]),
        ("swap", grid.at[:, 0, :, :, pl.ds(0, 3)]),
    ):
        copies.sent(kind, every, partner)

    @pl.when(moved)
    def _():
        copies.sent("turned", turned_in, partner)
        copies.sent("rows", link_rows, partner)


def deliver(*refs):
    sems = refs[-1]
    moves = [pltpu.make_async_copy(refs[at], refs[4 + at], sems.at[at]) for at in range(4)]
    for move in moves:
        move.start()
    for move in moves:
        move.wait()


def body(*arrays):
    *arrays, ancestors = arrays
    vmem = pl.BlockSpec(memory_space=pltpu.VMEM)
    hbm = pl.BlockSpec(memory_space=pltpu.HBM)
    shape = jax.ShapeDtypeStruct
    sizes = ((B, B), (B, B), (H, B), (B, B))
    held = pl.pallas_call(
        kernel,
        out_shape=tuple(pltpu.VMEM(size, F32) for size in sizes),
        in_specs=[hbm] * 6,
        out_specs=(vmem,) * 4,
        scratch_shapes=[
            pltpu.SMEM((2, 32), jnp.int32),
            pltpu.VMEM((B, 4 * B), F32),
            pltpu.VMEM((4 * B, B), F32),
            pltpu.VMEM((B, B), F32),
            pltpu.VMEM((B, B), F32),
            pltpu.VMEM((B, B), F32),
            pltpu.SemaphoreType.DMA((12,)),
            pltpu.VMEM((B, 4 * B), BF16),
            pltpu.VMEM((B, 4 * B), BF16),
            pltpu.VMEM((CH, 4 * B, 2 * W), BF16),
            pltpu.VMEM((B, 2 * B), BF16),
            pltpu.VMEM((B, B), BF16),
            pltpu.VMEM((B, B), BF16),
            pltpu.VMEM((CH, 4, 2, H, W), F32),
            pltpu.VMEM((CH, 3, 2, H, W), F32),
            pltpu.VMEM((CH, 2, H, W), F32),
            pltpu.VMEM((CH, 2, H, W), F32),
            pltpu.VMEM((CH, 4, 2, H, W), F32),
            pltpu.VMEM((4, 4, 2, H, B), F32),
            pltpu.VMEM((4, 4, H, B), F32),
            pltpu.VMEM((2, 2, H, B), F32),
            pltpu.VMEM((2, 2, H, B), F32),
            pltpu.VMEM((2, 2, H, B), F32),
            pltpu.VMEM((4, H, B), F32),
            pltpu.VMEM((3, H, B), F32),
            pltpu.VMEM((CH, H, W), F32),
            pltpu.VMEM((8, H, B), F32),
            pltpu.VMEM((H, B), F32),
            pltpu.VMEM((W, B), F32),
            pltpu.VMEM((CH, 2, 3, S, W), F32),
            pltpu.VMEM((CH, 3, S, W), F32),
            pltpu.VMEM((CH, 3, S, W), F32),
            pltpu.VMEM((CH, 3, S, W), F32),
            pltpu.VMEM((CH, 8, S, W), F32),
            pltpu.VMEM((CH, 2, 4, 2, 4, S, W), F32),
            pltpu.SemaphoreType.DMA((SENDS,)),
            pltpu.SemaphoreType.DMA((RECVS,)),
        ],
        compiler_params=pltpu.CompilerParams(
            collective_id=0, has_side_effects=True, vmem_limit_bytes=44 * 1024 * 1024
        ),
    )(*[pltpu.with_memory_space_constraint(given, pltpu.HBM) for given in (ancestors, *arrays)])
    held = [pltpu.with_memory_space_constraint(made, pltpu.VMEM) for made in held]
    return pl.pallas_call(
        deliver,
        out_shape=tuple(shape(size, F32) for size in sizes),
        in_specs=[vmem] * 4,
        out_specs=(hbm,) * 4,
        scratch_shapes=[pltpu.SemaphoreType.DMA((4,))],
    )(*held)


def solution(mesh):
    placed = (P("pcol", "prow"), P("prow", None), P("pcol", None), P(), P(), P())
    return jax.shard_map(
        body,
        mesh=mesh,
        in_specs=placed,
        out_specs=(P("pcol", None), P(), P(("prow", "pcol"), None), P()),
        check_vma=False,
    )
```

time: 65 us -> 58.5 us (0.900)
  Pallas kernels: 63.6 us -> 57.7 us
  local copies, waits for them, and re-layouts: 0.67 us -> 0 us
    pallas_call x1, Pallas kernels: 62.3 us -> 56.5 us  [body(): pl.pallas_call(kernel, out_shape=tuple((pltpu.VMEM(size, F32) for size in...]
    unnamed x2 -> x0, local copies, waits for them, and re-layouts: 0.67 us -> none
where the time goes in v4:
time: 58.5 us; the launch traced here: 58.4 us
  Pallas kernels  57.7 us (99%)
  between operations  0.64 us (1%)
    pallas_call x1, Pallas kernels, body(): pl.pallas_call(kernel, out_shape=tuple((pltpu.VMEM(size, F32) for size in...  56.5 us
    pallas_call x1, Pallas kernels, body(): pl.pallas_call(deliver, out_shape=tuple((shape(size, F32) for size in siz...  1.27 us

profile of v4, /device:TPU:1, one launch (start us, length us, event | category | flops | bytes accessed | tf_op | source)
XLA Modules:
  0.0 58.4 jit_solution(80041810042749835)
XLA Ops:
  0.6 56.5 %shard_map.93 = (f32[384,384]{1,0:T(8,128)S(1)}, f32[384,384]{1,0:T(8,128)S(1)}, f32[48,384]{1,0:T(8,128)S(1)}, f32[384,384]{1,0:T(8,128)S(1)}) custom-call(s32[2,32]{1,0:T(2,128)} %marks_hbm.1, f32[384,1536]{1,0:T(8,128)} %inv_hbm.1, f32[1536,384]{1,0:T(8,128)} %pan1_hbm.1, f32[384,384]{1,0:T(8,128)} %pan2_hbm.1, f32[384,384]{1,0:T(8,128)} %link_hbm.1, ...), custom_call_target="tpu_custom_call" | custom-call | tf_op jit(solution)/shard_map/pallas_call | solution.py:475
  57.1 1.3 %shard_map.94 = (f32[384,384]{1,0:T(8,128)}, f32[384,384]{1,0:T(8,128)}, f32[48,384]{1,0:T(8,128)}, f32[384,384]{1,0:T(8,128)}) custom-call(f32[384,384]{1,0:T(8,128)S(1)} %get-tuple-element.8.refs_0_, f32[384,384]{1,0:T(8,128)S(1)} %get-tuple-element.9.refs_1_, f32[48,384]{1,0:T(8,128)S(1)} %get-tuple-element.10.refs_2_, ...), custom_call_target="tpu_custom_call" | custom-call | tf_op jit(solution)/shard_map/pallas_call | solution.py:524

commit v5 on v4

--- a/solution.py
+++ b/solution.py
@@ -15,8 +15,8 @@
 W = 128
 H = 48
 S = 16
-SENDS = 14
-RECVS = 40
+SENDS = 13
+RECVS = 46
 ROWS = (((0,), (0,)), ((), ()))
 PLAIN = (((1,), (0,)), ((), ()))
 
@@ -61,8 +61,9 @@
     def wait(self, key, every, device):
         self.make(key, every, every, device).wait_recv()
 
-    def sent(self, kind, every, device):
-        self.make((kind, 0), every, every, device).wait_send()
+    def sent(self, kind, every):
+        sem = self.send_sems.at[self.kinds[kind]]
+        pltpu.make_async_copy(every, every, sem).wait()
 
 
 class Ring:
@@ -133,7 +134,7 @@
     marks, inv, pan1, pan2, link, diag, load_sems, inv_high, inv_low, pan1_cat, pan2_cat, link_high, link_low,
     part, part_in, quarter, quarter_in, column,
     wide, wide_in, wide_relay, wide_direct, wide_final, mine, mine_in, link_rows,
-    turned, turned_in, cross, pair, pair_in, slices, slices_in, depth, grid,
+    turned, turned_in, cross, pair, slices_in, depth, grid,
     send_sems, recv_sems,
 ):
     row, col = lax.axis_index("prow"), lax.axis_index("pcol")
@@ -169,10 +170,14 @@
 
     partner = device(core=1 - core)
     opposite = at_z(turn(z, 4, 8))
-    after = (lax.div(col, 4), lax.rem(col, 4) * 8 + row)
-    before = (lax.rem(col, 8), row * 4 + lax.div(col, 8))
-    fixed = jnp.logical_and(after[0] == row, after[1] == col)
-    moved = jnp.logical_not(fixed)
+    def unless_me(there):
+        return jnp.logical_not(jnp.logical_and(there[0] == row, there[1] == col))
+
+    rows_to = (lax.div(col, 4), lax.rem(col, 4) * 8 + y * 2 + zh)
+    rows_from = (lax.rem(col, 2) * 4 + lax.div(lax.rem(col, 8), 2), row * 4 + lax.div(col, 8))
+    slice_to = (lax.rem(col, 8), row * 4 + lax.div(col, 8))
+    slice_from = (lax.div(col, 4), lax.rem(col, 4) * 8 + row)
+    rows_move, slice_move = unless_me(rows_to), unless_me(slice_to)
 
     barrier = pltpu.get_barrier_semaphore()
 
@@ -183,26 +188,47 @@
     for step in (1, 2, 3):
         greet(at_y(turn(y, step)))
         greet(at_x(turn(x, step)))
+        greet(device(x=turn(x, step), core=1 - core))
     greet(partner)
     for step in range(1, 8):
         greet(at_z(turn(z, step, 8)))
 
-    @pl.when(moved)
+    @pl.when(rows_move)
     def _():
-        greet(after)
-        greet(before)
-
-    for load in loads[:11]:
+        greet(rows_from)
+
+    @pl.when(slice_move)
+    def _():
+        greet(slice_from)
+
+    for load in loads[0:8:2] + loads[1:8:2]:
         load.start()
 
     copies = Copies(send_sems, recv_sems)
 
+    def permute(key, src, dst, there, moved):
+        remote = copies.make(key, src, dst, there)
+        local = pltpu.make_async_copy(src, dst, copies.recv_sem(key))
+
+        @pl.when(moved)
+        def _():
+            remote.start()
+
+        @pl.when(jnp.logical_not(moved))
+        def _():
+            local.start()
+
+    for load in loads[0:8:2]:
+        load.wait()
+
+    block = pan1[pl.ds(pl.multiple_of(lax.div(col, 8) * B, B), B), :]
+    turned[...] = block.T.reshape(8, H, B)
     loads[11].wait()
     first_own = marks[0, col].astype(F32)
     second_own = marks[1, col].astype(F32)
+    early = []
     for block in range(4):
-        at = pl.ds(block * B, B)
-        loads[2 * block].wait()
+        at = slice(block * B, (block + 1) * B)
         scaled = pan1[at, :] * marks[0, row * 4 + block].astype(F32)
         high, low = split(scaled)
         for chunk in range(CH):
@@ -211,6 +237,13 @@
             pan1_cat[chunk, at, W : 2 * W] = low[:, lanes]
         loads[2 * block + 1].wait()
         inv_high[:, at], inv_low[:, at] = split(inv[:, at])
+        both = mul(inv_high[:, at], pan1_cat[0, at, :])
+        rest = mul(inv_low[:, at], pan1_cat[0, at, 0:W])
+        early.append(both[:, 0:W] + (both[:, W : 2 * W] + rest))
+    total = ((early[0] + early[1]) + (early[2] + early[3])) * (-first_own)
+    part[0] = total.reshape(4, 2, H, W)
+    for load in loads[8:11]:
+        load.start()
 
     def partial_product(chunk):
         both = mul(inv_high[...], pan1_cat[chunk])
@@ -220,26 +253,28 @@
 
     scatter, gather, along_x, along_z, gather_x, gather_y = [], [], [], [], [], []
     for chunk in range(CH):
-        scatter.append(
-            Exchange(
-                copies, ("part", chunk), y, 4, at_y,
-                lambda there, k=chunk: part.at[k, there],
-                lambda step, k=chunk: part_in.at[k, step - 1],
-                part_in.at[chunk],
+        for half in range(2):
+            scatter.append(
+                Exchange(
+                    copies, ("part", chunk, half), y, 4, at_y,
+                    lambda there, k=chunk, h=half: part.at[k, there, h],
+                    lambda step, k=chunk, h=half: part_in.at[k, h, step - 1],
+                    part_in.at[chunk, half],
+                )
             )
-        )
-        gather.append(
-            Exchange(
-                copies, ("column", chunk), y, 4, at_y,
-                lambda there, k=chunk: column.at[k, y],
-                lambda step, k=chunk: column.at[k, y],
-                column.at[chunk, pl.ds(0, 3)],
+            gather.append(
+                Exchange(
+                    copies, ("column", chunk, half), y, 4, at_y,
+                    lambda there, k=chunk, h=half: column.at[k, y, h],
+                    lambda step, k=chunk, h=half: column.at[k, y, h],
+                    column.at[chunk, pl.ds(0, 3), half],
+                )
             )
-        )
         along_x.append(
             Exchange(
-                copies, ("slices", chunk), x, 4, at_x,
-                lambda there, k=chunk: slices.at[k, jnp.minimum(there, 2)],
+                copies, ("slices", chunk), x * 2 + core, 8,
+                lambda there: device(x=lax.div(there, 2), core=lax.rem(there, 2)),
+                lambda there, k=chunk: pair.at[k, lax.rem(there, 2), jnp.minimum(lax.div(there, 2), 2)],
                 lambda step, k=chunk: slices_in.at[k, step - 1],
                 slices_in.at[chunk],
             )
@@ -282,30 +317,17 @@
         mine_in,
     )
 
-    def permute(key, src, dst, there):
-        remote = copies.make(key, src, dst, there)
-        local = pltpu.make_async_copy(src, dst, copies.recv_sem(key))
-
-        @pl.when(moved)
-        def _():
-            remote.start()
-
-        @pl.when(fixed)
-        def _():
-            local.start()
-
-    partial_product(0)
-
-    block = pan1[pl.ds(pl.multiple_of(lax.div(col, 8) * B, B), B), :]
-    turned[...] = block.T.reshape(8, H, B)
-    pl.semaphore_wait(barrier, 14 + jnp.where(moved, 2, 0))
+    pl.semaphore_wait(barrier, 17 + jnp.where(rows_move, 1, 0) + jnp.where(slice_move, 1, 0))
     scatter[0].start()
+    scatter[1].start()
 
     partial_product(1)
-    scatter[1].start()
+    scatter[2].start()
+    scatter[3].start()
     partial_product(2)
-    scatter[2].start()
-
+    scatter[4].start()
+    scatter[5].start()
+    permute(("turned", 0), turned.at[lax.rem(col, 8)], turned_in, slice_to, slice_move)
     loads[8].wait()
     high, low = split(pan2[...] * second_own)
     pan2_cat[:, 0:B] = high
@@ -326,41 +348,44 @@
         for lo in range(4):
             wide[there, lo, core] = wide[there, lo, core] + wide_in[there, lo]
 
-    def to_opposite(chunk):
-        scatter[chunk].finish()
-        quarter[chunk] = (part[chunk, y] + part_in[chunk, 0]) + (part_in[chunk, 1] + part_in[chunk, 2])
-        copies.send(("half", chunk), quarter.at[chunk], quarter_in.at[chunk], opposite)
+    def to_opposite(chunk, half):
+        scatter[2 * chunk + half].finish()
+        quarter[chunk, half] = (part[chunk, y, half] + part_in[chunk, half, 0]) + (
+            part_in[chunk, half, 1] + part_in[chunk, half, 2]
+        )
+        copies.send(("half", chunk, half), quarter.at[chunk, half], quarter_in.at[chunk, half], opposite)
 
     wide_product(2)
+    to_opposite(0, 0)
+    to_opposite(0, 1)
     wide_product(1)
-    to_opposite(0)
-    wide_product(3)
-    to_opposite(1)
-    wide_product(0)
-    to_opposite(2)
-    permute(("turned", 0), turned.at[lax.rem(col, 8)], turned_in, before)
     wide_ready(2)
     across.start_far()
+    to_opposite(1, 0)
+    to_opposite(1, 1)
+    wide_product(3)
     wide_ready(1)
     across.start_plus()
+    to_opposite(2, 0)
+    to_opposite(2, 1)
+    wide_product(0)
     wide_ready(3)
     across.start_minus()
-    wide_ready(0)
     loads[9].wait()
     loads[10].wait()
     link_high[...], link_low[...] = split(link[...])
     for chunk in range(CH):
-        copies.wait(("half", chunk), quarter_in.at[chunk], opposite)
-        column[chunk, y] = quarter[chunk] + quarter_in[chunk]
-        gather[chunk].start()
-
-    across.relay()
+        for half in range(2):
+            copies.wait(("half", chunk, half), quarter_in.at[chunk, half], opposite)
+            column[chunk, y, half] = quarter[chunk, half] + quarter_in[chunk, half]
+            gather[2 * chunk + half].start()
 
     copies.wait(("turned", 0), turned_in, partner)
     turned_high, turned_low = split(turned_in[...])
 
     for chunk in range(CH):
-        gather[chunk].finish()
+        gather[2 * chunk].finish()
+        gather[2 * chunk + 1].finish()
         whole = column[chunk].reshape(B, W)
         column_first[:, chunk * W : (chunk + 1) * W] = whole
         whole = split(whole)
@@ -371,20 +396,19 @@
         pair[chunk, 0] = slice_first.reshape(3, S, W)
         for third in range(3):
             pair[chunk, 1, third] = cross[pl.ds(pl.multiple_of(row * S, S), S), third * W : (third + 1) * W]
-        copies.send(("pair", chunk), pair.at[chunk, 1 - core], pair_in.at[chunk], partner)
-    for chunk in range(CH):
-        copies.wait(("pair", chunk), pair_in.at[chunk], partner)
-        slices[chunk] = pair[chunk, core] + pair_in[chunk]
         along_x[chunk].start()
+        if chunk == 0:
+            wide_ready(0)
+            across.relay()
     for chunk in range(CH):
         along_x[chunk].finish()
-        depth[chunk, z] = (slices[chunk, jnp.minimum(x, 2)] + slices_in[chunk, 0]) + (
-            slices_in[chunk, 1] + slices_in[chunk, 2]
-        )
+        total = pair[chunk, core, jnp.minimum(x, 2)] + slices_in[chunk, 0]
+        for step in range(1, 7):
+            total = total + slices_in[chunk, step]
+        depth[chunk, z] = total
         along_z[chunk].start()
 
-    permute(("rows", 0), column.at[:, lax.div(row, 2), lax.rem(row, 2)], link_rows, after)
-
+    permute(("rows", 0), column.at[:, y, zh], link_rows, rows_to, rows_move)
     for chunk in range(CH):
         along_z[chunk].finish()
         for half in range(2):
@@ -442,19 +466,21 @@
         ("pairs", wide_in),
         ("wide", wide.at[pl.ds(0, 3), :, 0]),
         ("line", mine_in),
-        ("pair", pair_in),
         ("slices", slices_in),
         ("depth", depth.at[:, pl.ds(0, 7)]),
         ("grid_x", grid.at[:, 0, pl.ds(0, 3), :, 0]),
         ("grid_y", grid.at[:, 0, pl.ds(0, 3), :, pl.ds(0, 3)]),
         ("swap", grid.at[:, 0, :, :, pl.ds(0, 3)]),
     ):
-        copies.sent(kind, every, partner)
-
-    @pl.when(moved)
+        copies.sent(kind, every)
+
+    @pl.when(slice_move)
     def _():
-        copies.sent("turned", turned_in, partner)
-        copies.sent("rows", link_rows, partner)
+        copies.sent("turned", turned_in)
+
+    @pl.when(rows_move)
+    def _():
+        copies.sent("rows", link_rows)
 
 
 def deliver(*refs):
@@ -492,7 +518,7 @@
             pltpu.VMEM((B, B), BF16),
             pltpu.VMEM((B, B), BF16),
             pltpu.VMEM((CH, 4, 2, H, W), F32),
-            pltpu.VMEM((CH, 3, 2, H, W), F32),
+            pltpu.VMEM((CH, 2, 3, H, W), F32),
             pltpu.VMEM((CH, 2, H, W), F32),
             pltpu.VMEM((CH, 2, H, W), F32),
             pltpu.VMEM((CH, 4, 2, H, W), F32),
@@ -508,9 +534,7 @@
             pltpu.VMEM((H, B), F32),
             pltpu.VMEM((W, B), F32),
             pltpu.VMEM((CH, 2, 3, S, W), F32),
-            pltpu.VMEM((CH, 3, S, W), F32),
-            pltpu.VMEM((CH, 3, S, W), F32),
-            pltpu.VMEM((CH, 3, S, W), F32),
+            pltpu.VMEM((CH, 7, S, W), F32),
             pltpu.VMEM((CH, 8, S, W), F32),
             pltpu.VMEM((CH, 2, 4, 2, 4, S, W), F32),
             pltpu.SemaphoreType.DMA((SENDS,)),

time: 58.5 us -> 56.6 us (0.968)
  Pallas kernels: 57.7 us -> 55.6 us
    pallas_call x1, Pallas kernels: 56.5 us -> 54.3 us  [body(): pl.pallas_call(kernel, out_shape=tuple((pltpu.VMEM(size, F32) for size in...]
where the time goes in v5:
time: 56.6 us; the launch traced here: 56.2 us
  Pallas kernels  55.6 us (98%)
  between operations  0.64 us (1%)
    pallas_call x1, Pallas kernels, body(): pl.pallas_call(kernel, out_shape=tuple((pltpu.VMEM(size, F32) for size in...  54.3 us
    pallas_call x1, Pallas kernels, body(): pl.pallas_call(deliver, out_shape=tuple((shape(size, F32) for size in siz...  1.27 us

profile of v5, /device:TPU:1, one launch (start us, length us, event | category | flops | bytes accessed | tf_op | source)
XLA Modules:
  0.0 56.2 jit_solution(17205875283816121302)
XLA Ops:
  0.6 54.3 %shard_map.93 = (f32[384,384]{1,0:T(8,128)S(1)}, f32[384,384]{1,0:T(8,128)S(1)}, f32[48,384]{1,0:T(8,128)S(1)}, f32[384,384]{1,0:T(8,128)S(1)}) custom-call(s32[2,32]{1,0:T(2,128)} %marks_hbm.1, f32[384,1536]{1,0:T(8,128)} %inv_hbm.1, f32[1536,384]{1,0:T(8,128)} %pan1_hbm.1, f32[384,384]{1,0:T(8,128)} %pan2_hbm.1, f32[384,384]{1,0:T(8,128)} %link_hbm.1, ...), custom_call_target="tpu_custom_call" | custom-call | tf_op jit(solution)/shard_map/pallas_call | solution.py:501
  55.0 1.3 %shard_map.94 = (f32[384,384]{1,0:T(8,128)}, f32[384,384]{1,0:T(8,128)}, f32[48,384]{1,0:T(8,128)}, f32[384,384]{1,0:T(8,128)}) custom-call(f32[384,384]{1,0:T(8,128)S(1)} %get-tuple-element.8.refs_0_, f32[384,384]{1,0:T(8,128)S(1)} %get-tuple-element.9.refs_1_, f32[48,384]{1,0:T(8,128)S(1)} %get-tuple-element.10.refs_2_, ...), custom_call_target="tpu_custom_call" | custom-call | tf_op jit(solution)/shard_map/pallas_call | solution.py:548

commit v6 on v5

--- a/solution.py
+++ b/solution.py
@@ -417,9 +417,6 @@
             ) + depth[chunk, 4 * half + 3]
         gather_x[chunk].start()
 
-    mine[0:2], mine[2:4] = across.finish()
-    line.start()
-
     def pass_on(chunk, step):
         part_at = grid.at[chunk, core, turn(y, step), :, pl.ds(0, 3)]
         copies.send(("swap", chunk), part_at, part_at, partner)
@@ -428,6 +425,9 @@
         gather_x[chunk].finish()
         gather_y[chunk].start()
         pass_on(chunk, 0)
+    mine[0:2], mine[2:4] = across.finish()
+    line.start()
+
     for chunk in range(CH):
         gather_y[chunk].finish()
         for step in (1, 3, 2):

time: 56.6 us -> 56.6 us (level)
  no operation moved by 1% of the time
where the time goes in v6:
time: 56.6 us; the launch traced here: 56.5 us
  Pallas kernels  55.9 us (99%)
  between operations  0.64 us (1%)
    pallas_call x1, Pallas kernels, body(): pl.pallas_call(kernel, out_shape=tuple((pltpu.VMEM(size, F32) for size in...  54.6 us
    pallas_call x1, Pallas kernels, body(): pl.pallas_call(deliver, out_shape=tuple((shape(size, F32) for size in siz...  1.27 us

profile of v6, /device:TPU:1, one launch (start us, length us, event | category | flops | bytes accessed | tf_op | source)
XLA Modules:
  0.0 56.5 jit_solution(17988016607177480713)
XLA Ops:
  0.6 54.6 %shard_map.93 = (f32[384,384]{1,0:T(8,128)S(1)}, f32[384,384]{1,0:T(8,128)S(1)}, f32[48,384]{1,0:T(8,128)S(1)}, f32[384,384]{1,0:T(8,128)S(1)}) custom-call(s32[2,32]{1,0:T(2,128)} %marks_hbm.1, f32[384,1536]{1,0:T(8,128)} %inv_hbm.1, f32[1536,384]{1,0:T(8,128)} %pan1_hbm.1, f32[384,384]{1,0:T(8,128)} %pan2_hbm.1, f32[384,384]{1,0:T(8,128)} %link_hbm.1, ...), custom_call_target="tpu_custom_call" | custom-call | tf_op jit(solution)/shard_map/pallas_call | solution.py:501
  55.3 1.3 %shard_map.94 = (f32[384,384]{1,0:T(8,128)}, f32[384,384]{1,0:T(8,128)}, f32[48,384]{1,0:T(8,128)}, f32[384,384]{1,0:T(8,128)}) custom-call(f32[384,384]{1,0:T(8,128)S(1)} %get-tuple-element.8.refs_0_, f32[384,384]{1,0:T(8,128)S(1)} %get-tuple-element.9.refs_1_, f32[48,384]{1,0:T(8,128)S(1)} %get-tuple-element.10.refs_2_, ...), custom_call_target="tpu_custom_call" | custom-call | tf_op jit(solution)/shard_map/pallas_call | solution.py:548

commit v7 on v6

--- a/solution.py
+++ b/solution.py
@@ -408,9 +408,10 @@
         depth[chunk, z] = total
         along_z[chunk].start()
 
-    permute(("rows", 0), column.at[:, y, zh], link_rows, rows_to, rows_move)
     for chunk in range(CH):
         along_z[chunk].finish()
+        if chunk == 0:
+            permute(("rows", 0), column.at[:, y, zh], link_rows, rows_to, rows_move)
         for half in range(2):
             grid[chunk, core, y, half, x] = (
                 (depth[chunk, 4 * half] + depth[chunk, 4 * half + 1]) + depth[chunk, 4 * half + 2]

time: 56.6 us -> 57 us (level)
  no operation moved by 1% of the time
where the time goes in v7:
time: 57 us; the launch traced here: 56.5 us
  Pallas kernels  55.9 us (98%)
  between operations  0.64 us (1%)
    pallas_call x1, Pallas kernels, body(): pl.pallas_call(kernel, out_shape=tuple((pltpu.VMEM(size, F32) for size in...  54.6 us
    pallas_call x1, Pallas kernels, body(): pl.pallas_call(deliver, out_shape=tuple((shape(size, F32) for size in siz...  1.27 us

profile of v7, /device:TPU:1, one launch (start us, length us, event | category | flops | bytes accessed | tf_op | source)
XLA Modules:
  0.0 56.5 jit_solution(7063572000101362417)
XLA Ops:
  0.6 54.6 %shard_map.93 = (f32[384,384]{1,0:T(8,128)S(1)}, f32[384,384]{1,0:T(8,128)S(1)}, f32[48,384]{1,0:T(8,128)S(1)}, f32[384,384]{1,0:T(8,128)S(1)}) custom-call(s32[2,32]{1,0:T(2,128)} %marks_hbm.1, f32[384,1536]{1,0:T(8,128)} %inv_hbm.1, f32[1536,384]{1,0:T(8,128)} %pan1_hbm.1, f32[384,384]{1,0:T(8,128)} %pan2_hbm.1, f32[384,384]{1,0:T(8,128)} %link_hbm.1, ...), custom_call_target="tpu_custom_call" | custom-call | tf_op jit(solution)/shard_map/pallas_call | solution.py:502
  55.3 1.3 %shard_map.94 = (f32[384,384]{1,0:T(8,128)}, f32[384,384]{1,0:T(8,128)}, f32[48,384]{1,0:T(8,128)}, f32[384,384]{1,0:T(8,128)}) custom-call(f32[384,384]{1,0:T(8,128)S(1)} %get-tuple-element.8.refs_0_, f32[384,384]{1,0:T(8,128)S(1)} %get-tuple-element.9.refs_1_, f32[48,384]{1,0:T(8,128)S(1)} %get-tuple-element.10.refs_2_, ...), custom_call_target="tpu_custom_call" | custom-call | tf_op jit(solution)/shard_map/pallas_call | solution.py:549
